TPU v7x, 32 devices: a whole 2x2x4 slice. The times are simulated.
32 devices in a mesh: dp: 16 (over z, x, core), tensor: 2 (over y).
Axes of the slice: x: 2, y: 2, z: 4, core: 2. Of those that a mesh axis runs over, the one named last changes fastest.
Arguments:
- inputs: bfloat16 [12288, 768], P('dp'), may hold values from -6 to 6
- clip_ids: int32 [12288], replicated, may hold values from 0 to 11, never falling along the last dimension, each value on 1 to 1500 neighbouring positions
- attn_gain: bfloat16 [768], replicated, may hold values from 0.5 to 1.5
- attn_shift: bfloat16 [768], replicated, may hold values from -1.75 to 1.75
- w_query: bfloat16 [768, 768], P(None, 'tensor'), may hold values from -0.21875 to 0.21875
- query_bias: bfloat16 [768], P('tensor'), may hold values from -1.75 to 1.75
- w_key: bfloat16 [768, 768], P(None, 'tensor'), may hold values from -0.21875 to 0.21875
- w_value: bfloat16 [768, 768], P(None, 'tensor'), may hold values from -0.21875 to 0.21875
- value_bias: bfloat16 [768], P('tensor'), may hold values from -3 to 3
- w_out: bfloat16 [768, 768], P('tensor'), may hold values from -4 to 4
- out_bias: bfloat16 [768], replicated, may hold values from -1.75 to 1.75
- mlp_gain: bfloat16 [768], replicated, may hold values from 0.5 to 1.5
- mlp_shift: bfloat16 [768], replicated, may hold values from -1.75 to 1.75
- w_fc1: bfloat16 [768, 3072], P(None, 'tensor'), may hold values from -0.21875 to 0.21875
- fc1_bias: bfloat16 [3072], P('tensor'), may hold values from -3 to 3
- w_fc2: bfloat16 [3072, 768], P('tensor'), may hold values from -0.109375 to 0.109375
- fc2_bias: bfloat16 [768], replicated, may hold values from -1.75 to 1.75
- cotangent: bfloat16 [12288, 768], P('dp'), may hold values from -6 to 6
Outputs:
- layer_out: bfloat16 [12288, 768], P('dp')
- inputs_grad: float32 [12288, 768], P('dp')
- attn_gain_grad: float32 [768], replicated
- attn_shift_grad: float32 [768], replicated
- w_query_grad: float32 [768, 768], P(None, 'tensor')
- query_bias_grad: float32 [768], P('tensor')
- w_key_grad: float32 [768, 768], P(None, 'tensor')
- w_value_grad: float32 [768, 768], P(None, 'tensor')
- value_bias_grad: float32 [768], P('tensor')
- w_out_grad: float32 [768, 768], P('tensor')
- out_bias_grad: float32 [768], replicated
- mlp_gain_grad: float32 [768], replicated
- mlp_shift_grad: float32 [768], replicated
- w_fc1_grad: float32 [768, 3072], P(None, 'tensor')
- fc1_bias_grad: float32 [3072], P('tensor')
- w_fc2_grad: float32 [3072, 768], P('tensor')
- fc2_bias_grad: float32 [768], replicated
Inputs may be any that keep to these rules, and one draw needn't show every extreme that they name: `clip_ids`: clip numbers never fall along the tokens; each of the 12 clips holds 1 to 1500 consecutive tokens, and one holds exactly 1500.
All inputs are finite; a program needn't handle non-finite values.
Results may differ from a plain program's by a relative error of at most 0.012.
Values may be sent and summed in bfloat16 or wider, within the bound.
A program may use at most 128 MiB of HBM per device.

v0:
```python
import functools

import jax
import jax.numpy as jnp
from jax import lax
from jax.experimental import pallas as pl
from jax.experimental.pallas import tpu as pltpu
from jax.sharding import PartitionSpec as P

HEAD_DIM = 64
REACH = 2
TILE = 256
PIECES = 6
AHEAD = 2
NEG = -3e38
CLIPS = 64
LOGS = 64
CENTRES = 96
FAR = -(2.0**100)
SAFE = 40.0
BF = jnp.bfloat16
F32 = jnp.float32
MESH = pl.DeviceIdType.MESH
VMEM = pltpu.VMEM
VMEM_BYTES = 26_000_000
MID_BYTES = 50_000_000
FINISH_BYTES = 38_000_000
PARTS = 3
STRIP = 128
STRIPS = 3
DMA = pltpu.SemaphoreType.DMA


def dot_nn(left, right):
    return jnp.dot(left, right, preferred_element_type=F32)


def dot_tn(left, right):
    return lax.dot_general(left, right, (((0,), (0,)), ((), ())), preferred_element_type=F32)


def dot_nt(left, right):
    return lax.dot_general(left, right, (((1,), (1,)), ((), ())), preferred_element_type=F32)


def whole():
    return pl.BlockSpec(memory_space=VMEM)


def far():
    return pl.BlockSpec(memory_space=pltpu.HBM)


def in_hbm(value):
    return pltpu.with_memory_space_constraint(value, pltpu.HBM)


def remote(src, dst, send_sem, recv_sem, device):
    return pltpu.make_async_remote_copy(
        src_ref=src,
        dst_ref=dst,
        send_sem=send_sem,
        recv_sem=recv_sem,
        device_id=device,
        device_id_type=MESH,
    )


def place():
    d = lax.axis_index("dp")
    chip = d // 2
    core = d - 2 * chip
    has_left = chip > 0
    has_right = chip < lax.axis_size("dp") // 2 - 1
    return d, core, has_left, has_right


def greet(targets):
    barrier = pltpu.get_barrier_semaphore()
    count = 0
    for present, device in targets:
        if present is None:
            pl.semaphore_signal(barrier, inc=1, device_id=device, device_id_type=MESH)
            count = count + 1
        else:

            @pl.when(present)
            def _():
                pl.semaphore_signal(barrier, inc=1, device_id=device, device_id_type=MESH)

            count = count + present.astype(jnp.int32)
    pl.semaphore_wait(barrier, count)


def norm_rows(values):
    middle = jnp.mean(values, axis=-1, keepdims=True)
    centred = values - middle
    spread = jnp.mean(centred * centred, axis=-1, keepdims=True)
    return centred * lax.rsqrt(spread + 1e-05)


def halo_kernel(
    x_ref, wo_ref, wq_ref, wk_ref, wv_ref, vec_ref, lab_ref,
    q_ref, k_ref, v_ref, a_ref, wof_ref, n_ref, kc_ref,
    win, wq, wk, wv, load, sx, rx, sy, ry, ss, rs, sf, rf, sw, rw, sv, rv,
):
    d, core, has_left, has_right = place()
    t = lax.axis_index("tensor")
    height = x_ref.shape[0]
    cols = wq_ref.shape[1]
    half = height // 2
    piece = half // PIECES
    sibling = {"dp": d + 1 - 2 * core}
    across = {"tensor": 1 - t}
    exists = (has_left, has_right)
    slots = (0, 2 * REACH)
    part = wo_ref.shape[0] // 2
    wo_rows = pl.ds(pl.multiple_of(core * part, part), part)
    mine = pl.ds(pl.multiple_of(t * 2 * part, part), 2 * part)
    loads = [
        pltpu.make_async_copy(src, dst, load.at[i])
        for i, (src, dst) in enumerate(
            ((x_ref, win.at[REACH]), (wq_ref, wq), (wk_ref, wk), (wv_ref, wv), (wo_ref, wof_ref.at[mine]))
        )
    ]
    for copy in loads:
        copy.start()
    greet([(None, sibling), (None, across), (has_left, {"dp": d - 2}), (has_right, {"dp": d + 2})])

    def rows(which, p):
        return pl.ds(pl.multiple_of(which * half + p * piece, piece), piece)

    def x_copy(side, p):
        return remote(
            x_ref.at[rows(t, p)], win.at[slots[side], rows(t, p)], sx.at[side, p], rx.at[side, p],
            {"dp": d + 2 if side == 0 else d - 2},
        )

    def y_copy(side, p):
        spot = win.at[slots[side], rows(t, p)]
        return remote(spot, spot, sy.at[side, p], ry.at[side, p], across)

    def f_copy(which, p):
        span = rows(t if which == 0 else 1 - t, p)
        return remote(
            win.at[4 - 4 * core, span], win.at[3 - 2 * core, span], sf.at[which, p], rf.at[which, p],
            sibling,
        )

    own_copy = remote(x_ref, win.at[1 + 2 * core], ss, rs, sibling)

    def full_rows(which):
        return pl.ds(pl.multiple_of((2 * which + core) * part, part), part)

    w_copy = remote(wo_ref.at[wo_rows], wof_ref.at[full_rows(t)], sw, rw, across)
    wf_copy = remote(wof_ref.at[full_rows(1 - t)], wof_ref.at[full_rows(1 - t)], sv, rv, sibling)

    def send(p):
        for side in (0, 1):

            @pl.when(exists[1 - side])
            def _():
                x_copy(side, p).start()

    for p in range(AHEAD):
        send(p)
    w_copy.start()
    own_copy.start()
    vec = vec_ref[...].astype(F32)
    gain, shift = vec[0:1], vec[1:2]
    query_bias, value_bias = vec[2:3, :cols], vec[2:3, cols:]
    n_ref[...] = jnp.zeros(n_ref.shape, F32)

    def code(r, carry):
        labels = jnp.transpose(jnp.broadcast_to(lab_ref[pl.ds(r, 1), :], (128, 128)))
        lane = lax.broadcasted_iota(jnp.int32, (128, 128), 1)
        far = jnp.where(labels == lane.astype(F32), 0.0, FAR)
        kc_ref[pl.ds(pl.multiple_of(r * 128, 128), 128), :] = jnp.where(lane < CLIPS, far, 1.0).astype(BF)
        return carry

    lax.fori_loop(0, lab_ref.shape[0], code, 0)

    def raise_norm(spot, values):
        for c in range(cols // 128):
            span = values[:, c * 128 : c * 128 + 128]
            norm = jnp.max(jnp.sum(span * span, axis=1, keepdims=True), axis=0, keepdims=True)
            n_ref[spot, :] = jnp.maximum(n_ref[spot, :], norm)

    def project(slot, start):
        spot = pl.ds(pl.multiple_of(start, half), half)
        attn = (norm_rows(win[slot, spot, :].astype(F32)) * gain + shift).astype(BF)
        out = pl.ds(pl.multiple_of(slot * height + start, half), half)

        @pl.when(slot == REACH)
        def _():
            a_ref[spot, :] = attn

        query = (dot_nn(attn, wq[...]) + query_bias) * HEAD_DIM**-0.5
        key = dot_nn(attn, wk[...])
        q_ref[out, :] = query.astype(BF)
        k_ref[out, :] = key.astype(BF)
        raise_norm(slice(0, 8), query)
        raise_norm(slice(8, 16), key)
        v_ref[out, :] = (dot_nn(attn, wv[...]) + value_bias).astype(BF)

    def pass_on(p):
        for side in (0, 1):

            @pl.when(exists[side])
            def _():
                x_copy(side, p).wait_recv()
                y_copy(side, p).start()

            @pl.when(jnp.logical_and(exists[side], core == 1 - side))
            def _():
                f_copy(0, p).start()

        if p + AHEAD < PIECES:
            send(p + AHEAD)

    for copy in loads:
        copy.wait()

    def half_block(i, carry):
        @pl.when(i == 2)
        def _():
            pass_on(0)
            w_copy.wait_recv()
            wf_copy.start()
            for p in range(1, PIECES // 2):
                pass_on(p)
            own_copy.wait_recv()

        @pl.when(i == 4)
        def _():
            for p in range(PIECES // 2, PIECES):
                pass_on(p)

        @pl.when(i == 6)
        def _():
            for p in range(PIECES):
                for side in (0, 1):

                    @pl.when(exists[side])
                    def _():
                        y_copy(side, p).wait_recv()

                    @pl.when(jnp.logical_and(exists[side], core == 1 - side))
                    def _():
                        f_copy(1, p).start()

        @pl.when(i == 8)
        def _():
            for side in (0, 1):

                @pl.when(jnp.logical_and(exists[side], core == side))
                def _():
                    for which in (0, 1):
                        for p in range(PIECES):
                            f_copy(which, p).wait_recv()

        stage = i // 2
        odd = i - 2 * stage
        left, right = has_left.astype(jnp.int32), has_right.astype(jnp.int32)
        near = (1 - core) * left + core * right
        outer = (1 - odd) * left + odd * right

        def pick(values):
            total = 0
            for index, value in enumerate(values):
                total = total + (stage == index).astype(jnp.int32) * value
            return total

        slot = pick((REACH, 3 - 2 * core, 4 * odd, 4 * odd, 1 + 2 * core))
        which = pick((odd, odd, t, 1 - t, odd))

        @pl.when(pick((1, 1, outer, outer, near)) == 1)
        def _():
            project(slot, which * half)

        return carry

    lax.fori_loop(0, 10, half_block, 0)
    wf_copy.wait_recv()
    for copy in (own_copy, w_copy, wf_copy):
        copy.wait_send()
    for p in range(PIECES):
        for side in (0, 1):

            @pl.when(exists[1 - side])
            def _():
                x_copy(side, p).wait_send()

            @pl.when(exists[side])
            def _():
                y_copy(side, p).wait_send()

            @pl.when(jnp.logical_and(exists[side], core == 1 - side))
            def _():
                f_copy(0, p).wait_send()
                f_copy(1, p).wait_send()


def halo_qkv(x, wo, wq, wk, wv, vec, labels):
    height, width = x.shape
    cols = wq.shape[1]
    blocks = 2 * REACH + 1
    shape = jax.ShapeDtypeStruct
    wide = shape((blocks * height, cols), BF)
    pair = DMA((2, PIECES))
    return pl.pallas_call(
        halo_kernel,
        out_shape=(
            wide, wide, wide, shape((height, width), BF), shape((2 * wo.shape[0], wo.shape[1]), BF),
            shape((16, 128), F32), shape((blocks * height, 128), BF),
        ),
        in_specs=[far()] * 5 + [whole()] * 2,
        out_specs=[whole()] * 7,
        scratch_shapes=[pltpu.VMEM((blocks, height, width), BF)]
        + [pltpu.VMEM(wq.shape, BF)] * 3
        + [DMA((5,)), pair, pair, pair, pair, DMA, DMA, pair, pair, DMA, DMA, DMA, DMA],
        compiler_params=pltpu.CompilerParams(
            collective_id=0, has_side_effects=True, vmem_limit_bytes=VMEM_BYTES
        ),
        name="halo_qkv",
    )(*[in_hbm(value) for value in (x, wo, wq, wk, wv)], vec, labels)


def split3(values):
    first = values.astype(BF).astype(F32)
    second = (values - first).astype(BF).astype(F32)
    return first, second, values - first - second


def code_tile(rows, keys_code):
    count = rows.shape[1]
    terms = split3(-rows)
    lane = lax.broadcasted_iota(jnp.int32, (128, count), 0)
    tall = jnp.zeros((128, count), F32)
    for h in range(8):
        for base, row in ((LOGS, h), (CENTRES, 8 + h)):
            for i in range(3):
                tall = jnp.where(lane == base + 3 * h + i, terms[i][row : row + 1], tall)
    wide = jnp.transpose(tall)
    column = lax.broadcasted_iota(jnp.int32, wide.shape, 1)
    same = jnp.logical_and(column < CLIPS, keys_code.astype(F32) == 0.0)
    return jnp.where(same, 1.0, wide).astype(BF)


def tile_at(j):
    return pl.ds(pl.multiple_of(j * TILE, TILE), TILE)


def lanes_of(c):
    return pl.ds(c * 128, 128)


def beside(left, right):
    return jnp.concatenate([left, right], axis=1)


def stacked_heads(values, codes):
    lower = lax.broadcasted_iota(jnp.int32, values.shape, 1) < HEAD_DIM
    none = jnp.zeros_like(values)
    return jnp.concatenate(
        [beside(jnp.where(lower, values, none), codes[0]), beside(jnp.where(lower, none, values), codes[1])],
        axis=0,
    )


def heads_out(turned):
    pair = jnp.concatenate([turned[:HEAD_DIM, :TILE], turned[HEAD_DIM:, TILE:]], axis=0)
    return jnp.transpose(pair)


def within(lane, start):
    return jnp.logical_and(lane >= start, lane < start + 3)


def attfinish_kernel(b_ref, q_ref, k_ref, v_ref, kc_ref, n_ref, o_ref, lse_ref, r_ref, m_ref, l_ref, acc_ref):
    height, cols = o_ref.shape
    pairs, tiles = cols // 128, height // TILE
    steep = jnp.logical_not(jnp.max(n_ref[0:8, :]) * jnp.max(n_ref[8:16, :]) <= SAFE * SAFE)
    lane = lax.broadcasted_iota(jnp.int32, (TILE, 128), 1)

    def groups(values):
        return values.reshape(TILE // 8, 8, values.shape[1])

    def one(i, carry):
        lo, hi = b_ref[0, i], b_ref[1, i]
        own = pl.ds(pl.multiple_of(REACH * height + i * TILE, TILE), TILE)
        same = jnp.logical_and(lane < CLIPS, kc_ref[own, :].astype(F32) == 0.0)
        code = jnp.where(same, 1.0, 0.0).astype(BF)
        for c in range(pairs):
            r_ref[c] = stacked_heads(q_ref[own, lanes_of(c)], (code, code))
        acc_ref[...] = jnp.zeros(acc_ref.shape, F32)
        l_ref[...] = jnp.zeros(l_ref.shape, F32)
        m_ref[...] = jnp.zeros(m_ref.shape, F32)

        def score(j, c):
            return dot_nt(beside(k_ref[tile_at(j), lanes_of(c)], kc_ref[tile_at(j), :]), r_ref[c])

        def step(shift, j, carry):
            raised = []
            for c in range(pairs):
                s = score(j, c)
                e = jnp.exp(s - m_ref[c, 0:1, :] if shift else s)
                l_ref[c] += jnp.sum(groups(e), axis=0)
                raised.append(e.astype(BF))
            for c in range(pairs):
                acc_ref[c] += dot_tn(v_ref[tile_at(j), lanes_of(c)], raised[c])
            return carry

        @pl.when(jnp.logical_not(steep))
        def _():
            lax.fori_loop(lo, hi, functools.partial(step, False), 0)

        @pl.when(steep)
        def _():
            m_ref[...] = jnp.full(m_ref.shape, NEG, F32)

            def peak(j, carry):
                for c in range(pairs):
                    m_ref[c] = jnp.maximum(m_ref[c], jnp.max(groups(score(j, c)), axis=0))
                return carry

            lax.fori_loop(lo, hi, peak, 0)
            for c in range(pairs):
                m_ref[c] = jnp.broadcast_to(jnp.max(m_ref[c], axis=0, keepdims=True), m_ref.shape[1:])
            lax.fori_loop(lo, hi, functools.partial(step, True), 0)

        for c in range(pairs):
            total = jnp.sum(l_ref[c], axis=0, keepdims=True)
            o_ref[tile_at(i), lanes_of(c)] = heads_out(acc_ref[c] / total).astype(BF)
            logs = m_ref[c, 0:1, :] + jnp.log(total)
            lse_ref[2 * c : 2 * c + 1, tile_at(i)] = logs[:, :TILE]
            lse_ref[2 * c + 1 : 2 * c + 2, tile_at(i)] = logs[:, TILE:]
        return carry

    lse_ref[...] = jnp.zeros(lse_ref.shape, F32)
    lax.fori_loop(0, tiles, one, 0)


def local_call(kernel, name, out_shape, scratch, bounds, *values):
    grid = pltpu.PrefetchScalarGridSpec(
        num_scalar_prefetch=1,
        grid=(1,),
        in_specs=[whole()] * len(values),
        out_specs=jax.tree.map(lambda _: whole(), out_shape),
        scratch_shapes=scratch,
    )
    return pl.pallas_call(
        kernel,
        grid_spec=grid,
        out_shape=out_shape,
        compiler_params=pltpu.CompilerParams(vmem_limit_bytes=VMEM_BYTES),
        name=name,
    )(bounds, *values)


def attend(bounds, q, k, v, kc, norms, height):
    cols = k.shape[1]
    pairs = cols // 128
    out_shape = (jax.ShapeDtypeStruct((height, cols), BF), jax.ShapeDtypeStruct((8, height), F32))
    scratch = [
        pltpu.VMEM((pairs, 2 * TILE, 256), BF),
        pltpu.VMEM((pairs, 8, 2 * TILE), F32),
        pltpu.VMEM((pairs, 8, 2 * TILE), F32),
        pltpu.VMEM((pairs, 128, 2 * TILE), F32),
    ]
    return local_call(attfinish_kernel, "attend", out_shape, scratch, bounds, q, k, v, kc, norms)


def query_back_kernel(b_ref, q_ref, k_ref, v_ref, g_ref, kc_ref, qc_ref, dq_ref, r_ref, t_ref, acc_ref):
    height, cols = dq_ref.shape
    pairs, tiles = cols // 128, height // TILE
    lane = lax.broadcasted_iota(jnp.int32, (TILE, 128), 1)

    def one(i, carry):
        own = pl.ds(pl.multiple_of(REACH * height + i * TILE, TILE), TILE)
        code = qc_ref[own, :]
        none = jnp.zeros_like(code)
        for c in range(pairs):
            logs, centres = [], []
            for h in (2 * c, 2 * c + 1):
                logs.append(jnp.where(jnp.logical_or(lane < CLIPS, within(lane, LOGS + 3 * h)), code, none))
                centres.append(jnp.where(within(lane, CENTRES + 3 * h), code, none))
            r_ref[c] = stacked_heads(q_ref[own, lanes_of(c)], logs)
            t_ref[c] = stacked_heads(g_ref[own, lanes_of(c)], centres)
        acc_ref[...] = jnp.zeros(acc_ref.shape, F32)

        def step(j, carry):
            code = kc_ref[tile_at(j), :]
            steps = []
            for c in range(pairs):
                probs = jnp.exp(dot_nt(beside(k_ref[tile_at(j), lanes_of(c)], code), r_ref[c]))
                d_probs = dot_nt(beside(v_ref[tile_at(j), lanes_of(c)], code), t_ref[c])
                steps.append((probs * d_probs).astype(BF))
            for c in range(pairs):
                acc_ref[c] += dot_tn(k_ref[tile_at(j), lanes_of(c)], steps[c])
            return carry

        lax.fori_loop(b_ref[0, i], b_ref[1, i], step, 0)
        for c in range(pairs):
            dq_ref[tile_at(i), lanes_of(c)] = (heads_out(acc_ref[c]) * HEAD_DIM**-0.5).astype(BF)
        return carry

    lax.fori_loop(0, tiles, one, 0)


def query_back(bounds, q, k, v, g, kc, qc, height):
    cols = k.shape[1]
    pairs = cols // 128
    scratch = [pltpu.VMEM((pairs, 2 * TILE, 256), BF)] * 2 + [pltpu.VMEM((pairs, 128, 2 * TILE), F32)]
    out_shape = jax.ShapeDtypeStruct((height, cols), BF)
    return local_call(query_back_kernel, "query_back", out_shape, scratch, bounds, q, k, v, g, kc, qc)


def key_back_kernel(b_ref, q_ref, k_ref, v_ref, g_ref, kc_ref, qc_ref, dk_ref, dv_ref, r_ref, t_ref, ak_ref, av_ref):
    height, cols = dk_ref.shape
    pairs, tiles = cols // 128, height // TILE
    lane = lax.broadcasted_iota(jnp.int32, (TILE, 128), 1)

    def one(i, carry):
        own = pl.ds(pl.multiple_of(REACH * height + i * TILE, TILE), TILE)
        code = kc_ref[own, :]
        none, ones = jnp.zeros_like(code), jnp.ones_like(code)
        for c in range(pairs):
            logs, centres = [], []
            for h in (2 * c, 2 * c + 1):
                logs.append(jnp.where(lane < CLIPS, code, jnp.where(within(lane, LOGS + 3 * h), ones, none)))
                centres.append(jnp.where(within(lane, CENTRES + 3 * h), ones, none))
            r_ref[c] = stacked_heads(k_ref[own, lanes_of(c)], logs)
            t_ref[c] = stacked_heads(v_ref[own, lanes_of(c)], centres)
        ak_ref[...] = jnp.zeros(ak_ref.shape, F32)
        av_ref[...] = jnp.zeros(av_ref.shape, F32)

        def step(j, carry):
            code = qc_ref[tile_at(j), :]
            weights, steps = [], []
            for c in range(pairs):
                probs = jnp.exp(dot_nt(beside(q_ref[tile_at(j), lanes_of(c)], code), r_ref[c]))
                d_probs = dot_nt(beside(g_ref[tile_at(j), lanes_of(c)], code), t_ref[c])
                weights.append(probs.astype(BF))
                steps.append((probs * d_probs).astype(BF))
            for c in range(pairs):
                av_ref[c] += dot_tn(g_ref[tile_at(j), lanes_of(c)], weights[c])
                ak_ref[c] += dot_tn(q_ref[tile_at(j), lanes_of(c)], steps[c])
            return carry

        lax.fori_loop(b_ref[0, i], b_ref[1, i], step, 0)
        for c in range(pairs):
            dk_ref[tile_at(i), lanes_of(c)] = heads_out(ak_ref[c]).astype(BF)
            dv_ref[tile_at(i), lanes_of(c)] = heads_out(av_ref[c]).astype(BF)
        return carry

    lax.fori_loop(0, tiles, one, 0)


def key_back(bounds, q, k, v, g, kc, qc, height):
    cols = k.shape[1]
    pairs = cols // 128
    scratch = [pltpu.VMEM((pairs, 2 * TILE, 256), BF)] * 2 + [pltpu.VMEM((pairs, 128, 2 * TILE), F32)] * 2
    out_shape = (jax.ShapeDtypeStruct((height, cols), BF),) * 2
    return local_call(key_back_kernel, "key_back", out_shape, scratch, bounds, q, k, v, g, kc, qc)


class Ring:
    def __init__(self):
        d = lax.axis_index("dp")
        n = lax.axis_size("dp") // 2
        chip = d // 2
        core = d - 2 * chip
        odd = chip - 2 * (chip // 2)
        spot = (1 - odd) * (chip // 2) + odd * (n - 1 - chip // 2)
        self.here = (1 - core) * spot + core * (n - 1 - spot)
        self.n, self.core, self.hops = n, core, n // 2
        self.sibling = {"dp": d + 1 - 2 * core}
        self.after = {"dp": self.device_at(self.wrap(self.here + 1))}
        self.before = {"dp": self.device_at(self.wrap(self.here - 1))}

    def wrap(self, index):
        return lax.rem(index + 2 * self.n, self.n)

    def device_at(self, rank):
        n, core = self.n, self.core
        walk = (1 - core) * rank + core * (n - 1 - rank)
        late = walk // (n // 2)
        return 2 * ((1 - late) * (2 * walk) + late * (2 * (n - walk) - 1)) + core

    def spans(self, shape, i, owner, j):
        rows, cols = shape[0] // 2, shape[1]
        wide = STRIPS * STRIP
        high, count = rows * cols // (self.n * wide), cols // wide
        line = j // count
        row = pl.multiple_of(owner * rows + line * high, high)
        col = pl.multiple_of((j - line * count) * wide + i * STRIP, STRIP)
        return pl.ds(row, high), pl.ds(col, STRIP)


def units(arrays):
    return [(a, i, pl.ds(i * STRIP, STRIP), a * STRIPS + i) for a in range(arrays) for i in range(STRIPS)]


class Reduce:
    def __init__(self, ring, given, sibs, bufs, sems):
        self.ring, self.given, self.sibs, self.bufs, self.sems = ring, given, sibs, bufs, sems
        self.units = units(len(given))

    def s_copy(self, a):
        rows = self.given[a].shape[0] // 2
        span = pl.ds(pl.multiple_of((1 - self.ring.core) * rows, rows), rows)
        return remote(
            self.given[a].at[span], self.sibs[a], self.sems[0].at[a], self.sems[1].at[a], self.ring.sibling
        )

    def ways(self):
        ring = self.ring
        return (
            (0, ring.hops, lambda s: ring.wrap(ring.here + ring.hops - s), ring.after),
            (ring.hops + 1, ring.hops - 1, lambda s: ring.wrap(ring.here - ring.hops + 1 + s), ring.before),
        )

    def r_copy(self, u, way, s):
        a, _, strip, e = u
        base, _, _, target = way
        k = (s if base == 0 else self.ring.hops + s)
        src, dst = self.bufs[a].at[base + s, :, strip], self.bufs[a].at[base + s + 1, :, strip]
        return remote(src, dst, self.sems[2].at[e, k], self.sems[3].at[e, k], target)

    def terms(self, u, j):
        a, i, _, _ = u
        shape, core = self.given[a].shape, self.ring.core
        mine = self.given[a][self.ring.spans(shape, i, core, j)].astype(F32)
        return mine + self.sibs[a][self.ring.spans(shape, i, 0, j)].astype(F32)

    def swap(self, a):
        self.s_copy(a).start()

    def first(self, a):
        self.s_copy(a).wait_recv()
        for u in self.units:
            if u[0] == a:
                for way in self.ways():
                    self.bufs[a][way[0], :, u[2]] = self.terms(u, way[2](0)).astype(BF)
                    self.r_copy(u, way, 0).start()

    def step(self, s, both=True):
        for u in self.units:
            a, _, strip, _ = u
            for way in self.ways()[: 2 if both else 1]:
                slot = way[0] + s
                local = self.terms(u, way[2](s))
                self.r_copy(u, way, s - 1).wait_recv()
                self.bufs[a][slot, :, strip] = (self.bufs[a][slot, :, strip].astype(F32) + local).astype(BF)
                self.r_copy(u, way, s).start()

    def turn(self):
        hops = self.ring.hops
        for u in self.units:
            a, _, strip, _ = u
            local = self.terms(u, self.ring.here)
            ahead, back = self.ways()
            self.r_copy(u, back, hops - 2).wait_recv()
            local = local + self.bufs[a][2 * hops, :, strip].astype(F32)
            self.r_copy(u, ahead, hops - 1).wait_recv()
            self.bufs[a][hops, :, strip] = (self.bufs[a][hops, :, strip].astype(F32) + local).astype(BF)

    def settle(self):
        for a in range(len(self.given)):
            self.s_copy(a).wait_send()
        for way in self.ways():

            def step(s, carry):
                for u in self.units:
                    self.r_copy(u, way, s).wait_send()
                return carry

            lax.fori_loop(0, way[1], step, 0)


class Gather:
    def __init__(self, ring, outs, sems):
        self.ring, self.outs, self.sems = ring, outs, sems
        self.units = units(len(outs))

    def spot(self, u, j):
        out, ring = self.outs[u[0]], self.ring
        return out.at[ring.spans(out.shape, u[1], ring.core, ring.wrap(ring.here + j))]

    def g_copy(self, u, way, s):
        ring = self.ring
        spot = self.spot(u, -s if way == 0 else s)
        k = s if way == 0 else ring.hops + s
        target = ring.after if way == 0 else ring.before
        return remote(spot, spot, self.sems[0].at[u[3], k], self.sems[1].at[u[3], k], target)

    def c_copy(self, u, way, s):
        spot = self.spot(u, -s if way == 0 else s)
        k = s if way == 0 else self.ring.hops + s
        return remote(spot, spot, self.sems[2].at[u[3], k], self.sems[3].at[u[3], k], self.ring.sibling)

    def begin(self, sources):
        for u in self.units:
            a, _, strip, _ = u
            self.spot(u, 0)[...] = sources[a][:, strip]
            self.g_copy(u, 0, 0).start()
            self.g_copy(u, 1, 0).start()
            self.c_copy(u, 0, 0).start()

    def step(self, s):
        for u in self.units:
            for way in (0, 1):
                self.g_copy(u, way, s - 1).wait_recv()
                self.g_copy(u, way, s).start()
                self.c_copy(u, way, s).start()

    def last(self):
        hops = self.ring.hops
        for u in self.units:
            self.g_copy(u, 0, hops - 2).wait_recv()
            self.g_copy(u, 0, hops - 1).start()
            self.c_copy(u, 0, hops - 1).start()
            self.g_copy(u, 1, hops - 2).wait_recv()
            self.c_copy(u, 1, hops - 1).start()
        for u in self.units:
            self.g_copy(u, 0, hops - 1).wait_recv()
            self.c_copy(u, 0, hops).start()

    def settle(self):
        hops = self.ring.hops
        for way in (0, 1):

            def sent(s, carry):
                for u in self.units:
                    self.g_copy(u, way, s).wait_send()
                return carry

            def copied(s, carry):
                for u in self.units:
                    self.c_copy(u, way, s).wait()
                return carry

            lax.fori_loop(0, hops - way, sent, 0)
            lax.fori_loop(way, hops + 1 - way, copied, 0)


def between(step, done, hops):
    def body(s, carry):
        step(s)
        return carry

    if done < hops - 1:
        lax.fori_loop(done, hops - 1, body, 0)


def chunk_rows(shape, n):
    return shape[0] * shape[1] // (2 * n * STRIPS * STRIP)


def reduce_scratch(shapes, n):
    count = len(shapes)
    sibs = [pltpu.VMEM((rows // 2, cols), BF) for rows, cols in shapes]
    bufs = [pltpu.VMEM((n + 1, chunk_rows(shape, n), STRIPS * STRIP), BF) for shape in shapes]
    return sibs + bufs, [DMA((count,))] * 2 + [DMA((count * STRIPS, n - 1))] * 2


def gather_sems(count, n):
    return [DMA((count * STRIPS, n - 1))] * 2 + [DMA((count * STRIPS, n))] * 2


def norm_back_rows(grad, values, gain):
    middle = jnp.mean(values, axis=-1, keepdims=True)
    centred = values - middle
    inverse = lax.rsqrt(jnp.mean(centred * centred, axis=-1, keepdims=True) + 1e-05)
    n = centred * inverse
    t = grad * gain
    back = (t - jnp.mean(t, axis=-1, keepdims=True) - n * jnp.mean(t * n, axis=-1, keepdims=True)) * inverse
    return back, grad * n


def column_sums(values):
    return jnp.sum(values, axis=0, keepdims=True)


def mid_kernel(
    x_ref, cot_ref, mix_ref, lse_ref, kc_ref, wof_ref, row_ref, w1_ref, w2_ref,
    xw_ref, qc_ref, rg_ref, low_ref, vec_ref, own1_ref, own2_ref, res_ref, outp_ref,
    om_ref, dact_ref, mi_ref, act_ref, pg_ref, part_ref, oth_ref, f1_ref, f2_ref, st_ref, sw_ref,
    sib1, sib2, buf1, buf2,
    sm, rm, sy, ry, sx, rx, ss, rs, sf, rf, *ring_sems,
):
    d, core, has_left, has_right = place()
    t = lax.axis_index("tensor")
    height, cols = mix_ref.shape
    width, hidden = w1_ref.shape
    rows = height // PARTS
    sibling = {"dp": d + 1 - 2 * core}
    across = {"tensor": 1 - t}
    exists = (has_left, has_right)
    slots = (0, 2 * REACH)
    ring = Ring()
    reduce = Reduce(ring, (f1_ref, f2_ref), (sib1, sib2), (buf1, buf2), ring_sems)
    hops = ring.hops
    greet([
        (None, sibling), (None, across), (has_left, {"dp": d - 2}), (has_right, {"dp": d + 2}),
        (None, ring.after), (None, ring.before),
    ])

    def span(p):
        return pl.ds(pl.multiple_of(p * rows, rows), rows)

    def m_copy(p):
        return remote(mix_ref.at[span(p)], om_ref.at[span(p)], sm.at[p], rm.at[p], across)

    def y_copy(p):
        return remote(part_ref.at[span(p)], oth_ref.at[span(p)], sy.at[p], ry.at[p], across)

    def refs(p):
        if p == PARTS:
            return st_ref, lambda slot: sw_ref.at[slot]
        return xw_ref.at[REACH, span(p)], lambda slot: xw_ref.at[slot, span(p)]

    def x_copy(side, p):
        src, dst = refs(p)
        return remote(
            src, dst(slots[side]), sx.at[side, p], rx.at[side, p],
            {"dp": d + 2 if side == 0 else d - 2},
        )

    def s_copy(p):
        src, dst = refs(p)
        return remote(src, dst(1 + 2 * core), ss.at[p], rs.at[p], sibling)

    def f_copy(p):
        _, dst = refs(p)
        return remote(dst(4 - 4 * core), dst(3 - 2 * core), sf.at[p], rf.at[p], sibling)

    def send(p):
        for side in (0, 1):

            @pl.when(exists[1 - side])
            def _():
                x_copy(side, p).start()

        s_copy(p).start()

    def pass_on(p):
        for side in (0, 1):

            @pl.when(exists[side])
            def _():
                x_copy(side, p).wait_recv()

            @pl.when(jnp.logical_and(exists[side], core == 1 - side))
            def _():
                f_copy(p).start()

    for p in range(PARTS):
        m_copy(p).start()
    vec = row_ref[...].astype(F32)
    out_bias, gain, shift = vec[3:4], vec[4:5], vec[5:6]
    heads = pl.ds(pl.multiple_of(t * cols, cols), cols)
    others = pl.ds(pl.multiple_of((1 - t) * cols, cols), cols)
    picks = lax.broadcasted_iota(jnp.int32, (8, cols), 1) // HEAD_DIM
    picks = (picks == lax.broadcasted_iota(jnp.int32, (8, cols), 0)).astype(F32)
    st_ref[0:8, :] = lse_ref[...]
    vec_ref[...] = jnp.zeros(vec_ref.shape, F32)

    def early(p, carry):
        cot = cot_ref[span(p), :]
        dact_ref[span(p), :] = dot_nt(cot, w2_ref[...])
        vec_ref[3:4, :] += column_sums(cot.astype(F32))
        res_ref[span(p), :] = x_ref[span(p), :].astype(F32) + dot_nn(mix_ref[span(p), :], wof_ref[heads, :]) + out_bias
        return carry

    lax.fori_loop(0, PARTS, early, 0)

    def forward(p, carry):
        m_copy(p).wait_recv()
        residual = res_ref[span(p), :] + dot_nn(om_ref[span(p), :], wof_ref[others, :])
        res_ref[span(p), :] = residual
        mlp_input = (norm_rows(residual) * gain + shift).astype(BF)
        mi_ref[span(p), :] = mlp_input
        for i in range(hidden // width):
            part = slice(i * width, (i + 1) * width)
            preact = dot_nn(mlp_input, w1_ref[:, part]) + vec[6 + i : 7 + i]
            cdf = 0.5 * (1.0 + lax.erf(preact * (2.0**-0.5)))
            pdf = jnp.exp(-0.5 * preact * preact) * 0.3989422804014327
            act_ref[span(p), part] = (preact * cdf).astype(BF)
            pre_grad = (dact_ref[span(p), part] * (cdf + preact * pdf)).astype(BF)
            pg_ref[span(p), part] = pre_grad
            vec_ref[4 + i : 5 + i, :] += column_sums(pre_grad.astype(F32))
        part_ref[span(p), :] = dot_nt(pg_ref[span(p), :], w1_ref[...]).astype(BF)
        y_copy(p).start()
        return carry

    lax.fori_loop(0, PARTS, forward, 0)

    def weights(which):
        half = pl.ds(pl.multiple_of(which * (width // 2), width // 2), width // 2)
        f1_ref[half, :] = dot_tn(mi_ref[:, half], pg_ref[...]).astype(BF)
        half = pl.ds(pl.multiple_of(which * (hidden // 2), hidden // 2), hidden // 2)
        f2_ref[half, :] = dot_tn(act_ref[:, half], cot_ref[...]).astype(BF)

    def back(p):
        y_copy(p).wait_recv()
        grad = part_ref[span(p), :].astype(F32) + oth_ref[span(p), :].astype(F32)
        turned, scaled = norm_back_rows(grad, res_ref[span(p), :], gain)
        total = cot_ref[span(p), :].astype(F32) + turned
        low = total.astype(BF)
        rg_ref[span(p), :] = total
        low_ref[span(p), :] = low
        vec_ref[0:1, :] += column_sums(scaled)
        vec_ref[1:2, :] += column_sums(grad)
        vec_ref[2:3, :] += column_sums(low.astype(F32))
        mixed_grad = dot_nt(low, wof_ref[heads, :]).astype(BF)
        xw_ref[REACH, span(p), :] = mixed_grad
        product = mixed_grad.astype(F32) * mix_ref[span(p), :].astype(F32)
        st_ref[8:16, p * rows : (p + 1) * rows] = lax.dot_general(
            picks, product, (((1,), (1,)), ((), ())),
            precision=lax.Precision.HIGHEST, preferred_element_type=F32,
        )

    def code(slot):
        def step(i, carry):
            spot = pl.ds(pl.multiple_of(slot * height + i * TILE, TILE), TILE)
            stats = sw_ref[slot, :, pl.ds(pl.multiple_of(i * TILE, TILE), TILE)]
            qc_ref[spot, :] = code_tile(stats, kc_ref[spot, :])
            return carry

        lax.fori_loop(0, height // TILE, step, 0)

    def ring_step(s):
        if s < hops - 1:
            reduce.step(s)

    back(0)
    send(0)
    weights(1 - core)
    reduce.swap(0)
    reduce.swap(1)
    back(1)
    send(1)
    weights(core)
    reduce.first(0)
    reduce.first(1)
    back(2)
    send(2)
    send(PARTS)
    sw_ref[REACH] = st_ref[...]
    ring_step(1)
    pass_on(0)
    outp_ref[...] = dot_nn(act_ref[...], w2_ref[...]).astype(BF)
    ring_step(2)
    pass_on(1)
    between(reduce.step, 3, hops)
    reduce.step(hops - 1, False)
    pass_on(2)
    pass_on(PARTS)
    code(REACH)
    reduce.turn()
    own1_ref[...] = buf1[hops]
    own2_ref[...] = buf2[hops]
    for p in range(PARTS + 1):
        s_copy(p).wait()
        for side in (0, 1):

            @pl.when(exists[1 - side])
            def _():
                x_copy(side, p).wait_send()

            @pl.when(jnp.logical_and(exists[side], core == 1 - side))
            def _():
                f_copy(p).wait_send()

            @pl.when(jnp.logical_and(exists[side], core == side))
            def _():
                f_copy(p).wait_recv()

    code(3 - 2 * core)
    for side in (0, 1):

        @pl.when(exists[side])
        def _():
            code(slots[side])

        @pl.when(jnp.logical_and(exists[side], core == side))
        def _():
            code(1 + 2 * core)

    for p in range(PARTS):
        m_copy(p).wait_send()
        y_copy(p).wait_send()
    reduce.settle()


def mid(x, cot, mix, lse, kc, wof, vec, w1, w2):
    blocks = 2 * REACH + 1
    height, width = x.shape
    hidden = w1.shape[1]
    n = lax.axis_size("dp") // 2
    pair, line, some = DMA((2, PARTS + 1)), DMA((PARTS + 1,)), DMA((PARTS,))
    room, sems = reduce_scratch((w1.shape, w2.shape), n)
    shape = jax.ShapeDtypeStruct
    chunks = [shape((chunk_rows(w.shape, n), STRIPS * STRIP), BF) for w in (w1, w2)]
    return pl.pallas_call(
        mid_kernel,
        out_shape=(
            shape((blocks,) + mix.shape, BF), shape(kc.shape, BF), shape(x.shape, F32), shape(x.shape, BF),
            shape((16, width), F32), *chunks, shape(x.shape, F32), shape(x.shape, BF),
        ),
        in_specs=[whole()] * 9,
        out_specs=[whole()] * 9,
        scratch_shapes=[
            pltpu.VMEM(mix.shape, BF), pltpu.VMEM((height, hidden), F32), pltpu.VMEM(x.shape, BF),
            pltpu.VMEM((height, hidden), BF), pltpu.VMEM((height, hidden), BF), pltpu.VMEM(x.shape, BF),
            pltpu.VMEM(x.shape, BF), pltpu.VMEM(w1.shape, BF), pltpu.VMEM(w2.shape, BF),
            pltpu.VMEM((16, height), F32), pltpu.VMEM((blocks, 16, height), F32),
        ]
        + room
        + [some, some, some, some, pair, pair, line, line, line, line]
        + sems,
        compiler_params=pltpu.CompilerParams(
            collective_id=1, has_side_effects=True, vmem_limit_bytes=MID_BYTES
        ),
        name="mid",
    )(x, cot, mix, lse, kc, wof, vec, w1, w2)


def finish_kernel(
    rounds, dq_ref, dk_ref, dv_ref, wq_ref, wk_ref, wv_ref, a_ref, low_ref, o_ref, x_ref, rg_ref, row_ref, vec_ref,
    own1_ref, own2_ref, res_hbm, outp_hbm, outo_hbm,
    ig_ref, g_ref, vs_ref, g1_ref, g2_ref, lo_ref,
    part_ref, oth_ref, own_ref, send_ref, got_ref, res_ref, outp_ref, outo_ref, sib, buf,
    load, sy, ry, sd, rd, *ring_sems,
):
    d, core, _, _ = place()
    t = lax.axis_index("tensor")
    height, cols = dq_ref.shape
    width = x_ref.shape[1]
    piece = height // PIECES
    across = {"tensor": 1 - t}
    loads = [
        pltpu.make_async_copy(src, dst, load.at[i])
        for i, (src, dst) in enumerate(((res_hbm, res_ref), (outp_hbm, outp_ref), (outo_hbm, outo_ref)))
    ]
    for copy in loads:
        copy.start()
    ring = Ring()
    reduce = Reduce(ring, (own_ref,), (sib,), (buf,), ring_sems[:4])
    gather = Gather(ring, (g_ref,), ring_sems[4:8])
    wide = Gather(ring, (g1_ref, g2_ref), ring_sems[8:])
    hops = ring.hops
    partners = []
    for r in range(rounds):
        bit = (d // 2**r) - 2 * (d // 2 ** (r + 1))
        partners.append({"dp": d + 2**r * (1 - 2 * bit)})
    greet([(None, across), (None, ring.after), (None, ring.before)] + [(None, p) for p in partners])

    def y_copy(p):
        span = pl.ds(p * piece, piece)
        return remote(part_ref.at[span], oth_ref.at[span], sy.at[p], ry.at[p], across)

    def d_copy(r):
        return remote(send_ref.at[r], got_ref.at[r], sd.at[r], rd.at[r], partners[r])

    def share(p):
        span = pl.ds(p * piece, piece)
        part = dot_nt(dq_ref[span, :], wq_ref[...]) + dot_nt(dk_ref[span, :], wk_ref[...])
        part_ref[span, :] = (part + dot_nt(dv_ref[span, :], wv_ref[...])).astype(BF)

    def weights(which):
        span = pl.ds(pl.multiple_of(which * (width // 2), width // 2), width // 2)
        attn = a_ref[:, span]
        for i, ref in enumerate((dq_ref, dk_ref, dv_ref)):
            own_ref[span, i * cols : (i + 1) * cols] = dot_tn(attn, ref[...]).astype(BF)
        own_ref[span, 3 * cols : 4 * cols] = dot_tn(low_ref[:, span], o_ref[...]).astype(BF)

    def wide_step(s):
        if s < hops - 1:
            wide.step(s)

    for p in range(AHEAD):
        share(p)
        y_copy(p).start()
    wide.begin((own1_ref, own2_ref))
    weights(1 - core)
    reduce.swap(0)
    for p in range(AHEAD, PIECES):
        share(p)
    wide_step(1)
    weights(core)
    vec = row_ref[...].astype(F32)
    gain, fc2_bias = vec[0:1], vec[8:9]
    gains, shifts = [], []

    def back(p):
        span = pl.ds(p * piece, piece)
        y_copy(p).wait_recv()
        if p + AHEAD < PIECES:
            y_copy(p + AHEAD).start()
        grad = part_ref[span, :].astype(F32) + oth_ref[span, :].astype(F32)
        turned, scaled = norm_back_rows(grad, x_ref[span, :].astype(F32), gain)
        ig_ref[span, :] = rg_ref[span, :] + turned
        gains.append(column_sums(scaled))
        shifts.append(column_sums(grad))

    def reduce_step(s):
        if s < hops - 1:
            reduce.step(s)

    def gather_step(s):
        if s < hops - 1:
            gather.step(s)

    def layer_out(p):
        span = pl.ds(p * piece, piece)
        total = outp_ref[span, :].astype(F32) + outo_ref[span, :].astype(F32)
        lo_ref[span, :] = (res_ref[span, :] + total + fc2_bias).astype(BF)

    def double(s):
        if s < rounds:
            d_copy(s).wait_recv()
            total = send_ref[s] + got_ref[s]
            if s + 1 < rounds:
                send_ref[s + 1] = total
                d_copy(s + 1).start()
            else:
                vs_ref[...] = total

    reduce.first(0)
    back(0)
    wide_step(2)
    reduce_step(1)
    back(1)
    reduce_step(2)
    back(2)
    between(reduce.step, 3, hops)
    between(wide.step, 3, hops)
    reduce.step(hops - 1, False)
    back(3)
    wide.last()
    reduce.turn()
    gather.begin((buf.at[hops],))
    back(4)
    gather_step(1)
    back(5)
    send_ref[0] = vec_ref[...]
    send_ref[0, 6:7, 0:cols] = column_sums(dq_ref[...].astype(F32))
    send_ref[0, 6:7, cols : 2 * cols] = column_sums(dv_ref[...].astype(F32))
    send_ref[0, 7:8, :] = sum(gains[1:], gains[0])
    send_ref[0, 8:9, :] = sum(shifts[1:], shifts[0])
    d_copy(0).start()
    gather_step(2)
    for copy in loads:
        copy.wait()
    layer_out(0)
    double(0)
    layer_out(1)
    between(gather.step, 3, hops)
    double(1)
    layer_out(2)
    gather.last()
    double(2)
    layer_out(3)
    layer_out(4)
    layer_out(5)
    for s in range(3, rounds):
        double(s)
    for p in range(PIECES):
        y_copy(p).wait_send()
    for r in range(rounds):
        d_copy(r).wait_send()
    reduce.settle()
    wide.settle()
    gather.settle()


def finish(dq, dk, dv, wq, wk, wv, attn, low, o, x, rg, gain, vectors, own1, own2, res, outp, outo, shapes):
    height, cols = dq.shape
    width = x.shape[1]
    size = lax.axis_size("dp")
    rounds = size.bit_length() - 1
    n = size // 2
    weights = (width, 4 * cols)
    room, sems = reduce_scratch((weights,), n)
    shape = jax.ShapeDtypeStruct
    return pl.pallas_call(
        functools.partial(finish_kernel, rounds),
        out_shape=(
            shape((height, width), F32), shape(weights, BF), shape(vectors.shape, F32),
            *[shape(dims, BF) for dims in shapes], shape((height, width), BF),
        ),
        in_specs=[whole()] * 15 + [far()] * 3,
        out_specs=[whole()] * 6,
        scratch_shapes=[
            pltpu.VMEM((height, width), BF), pltpu.VMEM((height, width), BF), pltpu.VMEM(weights, BF),
            pltpu.VMEM((rounds,) + vectors.shape, F32), pltpu.VMEM((rounds,) + vectors.shape, F32),
            pltpu.VMEM((height, width), F32), pltpu.VMEM((height, width), BF), pltpu.VMEM((height, width), BF),
        ]
        + room
        + [DMA((3,)), DMA((PIECES,)), DMA((PIECES,)), DMA((rounds,)), DMA((rounds,))]
        + sems
        + gather_sems(1, n)
        + gather_sems(2, n),
        compiler_params=pltpu.CompilerParams(
            collective_id=2, has_side_effects=True, vmem_limit_bytes=FINISH_BYTES
        ),
        name="finish",
    )(dq, dk, dv, wq, wk, wv, attn, low, o, x, rg, gain, vectors, own1, own2, res, outp, outo)


def widen_kernel(a_ref, f1_ref, f2_ref, q_ref, k_ref, v_ref, o_ref, g1_ref, g2_ref):
    cols = q_ref.shape[1]
    for i, ref in enumerate((q_ref, k_ref, v_ref)):
        ref[...] = a_ref[:, i * cols : (i + 1) * cols].astype(F32)
    o_ref[...] = jnp.transpose(a_ref[:, 3 * cols :].astype(F32))
    g1_ref[...] = f1_ref[...].astype(F32)
    g2_ref[...] = f2_ref[...].astype(F32)


def widen(attn, f1, f2):
    width = attn.shape[0]
    cols, steps = attn.shape[1] // 4, width // 128
    shape = jax.ShapeDtypeStruct

    def block(array):
        return pl.BlockSpec((array.shape[0] // steps, array.shape[1]), lambda i: (i, 0))

    thin = shape((width, cols), F32)
    outs = (thin, thin, thin, shape((cols, width), F32), shape(f1.shape, F32), shape(f2.shape, F32))
    return pl.pallas_call(
        widen_kernel,
        grid=(steps,),
        out_shape=outs,
        in_specs=[block(attn), block(f1), block(f2)],
        out_specs=[block(thin)] * 3
        + [pl.BlockSpec((cols, 128), lambda i: (0, i)), block(f1), block(f2)],
        compiler_params=pltpu.CompilerParams(vmem_limit_bytes=VMEM_BYTES),
        name="widen",
    )(attn, f1, f2)


def swapped(value):
    return lax.ppermute(value, "tensor", [(0, 1), (1, 0)])


def on_device(
    inputs, clip_ids, attn_gain, attn_shift, w_query, query_bias, w_key, w_value, value_bias,
    w_out, out_bias, mlp_gain, mlp_shift, w_fc1, fc1_bias, w_fc2, fc2_bias, cotangent,
):
    height = inputs.shape[0]
    d = lax.axis_index("dp")
    reach = REACH * height
    cols = w_query.shape[1]

    padded = jnp.pad(clip_ids, (reach, 0), constant_values=-1)
    padded = jnp.pad(padded, (0, reach), constant_values=1 << 20)
    window = lax.dynamic_slice_in_dim(padded, d * height, height + 2 * reach)
    own = window[reach : reach + height]
    firsts, lasts = own[::TILE], own[TILE - 1 :: TILE]
    begin = jnp.sum((window[None, :] < firsts[:, None]).astype(jnp.int32), axis=1)
    end = jnp.sum((window[None, :] <= lasts[:, None]).astype(jnp.int32), axis=1)
    bounds = jnp.stack([begin // TILE, (end + TILE - 1) // TILE])
    labels = window.astype(F32).reshape(-1, 128)
    split = jnp.pad(query_bias, (0, cols)) + jnp.pad(value_bias, (cols, 0))
    width = inputs.shape[1]
    rows = [attn_gain, attn_shift, split, out_bias, mlp_gain, mlp_shift, fc1_bias[:width], fc1_bias[width:], fc2_bias]
    line = lax.broadcasted_iota(jnp.int32, (16, width), 0)
    vec = jnp.zeros((16, width), BF)
    for i, values in enumerate(rows):
        vec = jnp.where(line == i, values[None, :], vec)

    q, k, v, attn_input, w_out_full, norms, key_code = halo_qkv(
        inputs, w_out, w_query, w_key, w_value, vec, labels
    )
    mixed, logs = attend(bounds, q, k, v, key_code, norms, height)
    grad_win, query_code, residual_grad, low, vectors, own1, own2, residual, out_part = mid(
        inputs, cotangent, mixed, logs, key_code, w_out_full, vec, w_fc1, w_fc2
    )
    grad_win = grad_win.reshape(-1, grad_win.shape[2])
    out_part, query_code = lax.optimization_barrier((out_part, query_code))
    out_other = swapped(out_part)
    query_low = query_back(bounds, q, k, v, grad_win, key_code, query_code, height)
    key_low, value_low = key_back(bounds, q, k, v, grad_win, key_code, query_code, height)
    out_other, key_low = lax.optimization_barrier((out_other, key_low))
    inputs_grad, attn_sum, sums, fc1_sum, fc2_sum, layer_out = finish(
        query_low, key_low, value_low, w_query, w_key, w_value, attn_input, low, mixed, inputs,
        residual_grad, vec, vectors, own1, own2, residual, out_part, out_other, (w_fc1.shape, w_fc2.shape),
    )
    q_grad, k_grad, v_grad, o_grad, fc1_grad, fc2_grad = widen(attn_sum, fc1_sum, fc2_sum)
    return (
        layer_out, inputs_grad, sums[7], sums[8],
        q_grad, sums[6, :cols], k_grad, v_grad, sums[6, cols:],
        o_grad, sums[2], sums[0], sums[1],
        fc1_grad, sums[4:6].reshape(-1), fc2_grad, sums[3],
    )


def solution(mesh):
    rows, cols, split, every = P("dp", None), P(None, "tensor"), P("tensor"), P()
    tall = P("tensor", None)
    in_specs = (
        rows, every, every, every, cols, split, cols, cols, split, tall, every, every, every,
        cols, split, tall, every, rows,
    )
    out_specs = (
        rows, rows, every, every, cols, split, cols, cols, split, tall, every, every, every,
        cols, split, tall, every,
    )
    return jax.shard_map(on_device, mesh=mesh, in_specs=in_specs, out_specs=out_specs, check_vma=False)
```

profile of v0, /device:TPU:0, one launch (start us, length us, event | category | flops | bytes accessed | tf_op | source)
XLA Modules:
  0.0 291.2 jit_solution(1062794180609514507)
XLA Ops:
  0.7 0.8 convert_bitcast_fusion
  2.0 0.8 fusion.2
  2.8 0.9 select_select_fusion.vec_ref.row_ref
  3.6 33.1 %halo_qkv.1 = (bf16[3840,384]{1,0:T(8,128)(2,1)S(1)}, bf16[3840,384]{1,0:T(8,128)(2,1)S(1)}, bf16[3840,384]{1,0:T(8,128)(2,1)S(1)}, bf16[768,768]{1,0:T(8,128)(2...) custom-call(bf16[768,768]{1,0:T(8,128)(2,1)} %x_ref.5, ...), custom_call_target="tpu_custom_call" | custom-call | tf_op jit(solution)/shard_map/halo_qkv/pallas_call | solution.py:311
  36.8 10.5 %attend.1 = (bf16[768,384]{1,0:T(8,128)(2,1)S(1)}, f32[8,768]{1,0:T(8,128)S(1)}) custom-call(s32[2,3]{1,0:T(2,128)S(1)} %pad_add_fusion.1.b_ref, bf16[3840,384]{1,0:T(8,128)(2,1)S(1)} %get-tuple-element.53.q_ref, bf16[3840,384]{1,0:T(8,128)(2,1)S(1)} %get-tuple-element.54.k_ref, bf16[3840,384]{1,0:T(8,128)(2,1)S(1)} %get-tuple-element.55.v_ref, ...), custom_call_target="tpu_custom_call" | custom-call | tf_op jit(solution)/shard_map/attend/pallas_call | solution.py:452
  47.3 101.2 %mid.1 = (bf16[5,768,384]{2,1,0:T(8,128)(2,1)}, bf16[3840,128]{1,0:T(8,128)(2,1)S(1)}, f32[768,768]{1,0:T(8,128)}, bf16[768,768]{1,0:T(8,128)(2,1)S(1)}, f32[16,...) custom-call(bf16[768,768]{1,0:T(8,128)(2,1)S(1)} %copy-done.1, ...), custom_call_target="tpu_custom_call" | custom-call | tf_op jit(solution)/shard_map/mid/pallas_call | solution.py:1007
  148.4 1.5 collective-permute-start
  149.9 1.8 copy-done
  151.7 13.6 %query_back.1.dq_ref = bf16[768,384]{1,0:T(8,128)(2,1)S(1)} custom-call(s32[2,3]{1,0:T(2,128)S(1)} %pad_add_fusion.1.b_ref, bf16[3840,384]{1,0:T(8,128)(2,1)S(1)} %get-tuple-element.53.q_ref, bf16[3840,384]{1,0:T(8,128)(2,1)S(1)} %get-tuple-element.54.k_ref, bf16[3840,384]{1,0:T(8,128)(2,1)S(1)} %get-tuple-element.55.v_ref, bf16[3840,384]{1,0:T(8,128)(2,1)S(1)} %bitcast.19, ...), custom_call_target="tpu_custom_call" | custom-call | tf_op jit(solution)/shard_map/query_back/pallas_call | solution.py:452
  165.4 14.9 %key_back.1 = (bf16[768,384]{1,0:T(8,128)(2,1)S(1)}, bf16[768,384]{1,0:T(8,128)(2,1)S(1)}) custom-call(s32[2,3]{1,0:T(2,128)S(1)} %pad_add_fusion.1.b_ref, bf16[3840,384]{1,0:T(8,128)(2,1)S(1)} %get-tuple-element.53.q_ref, bf16[3840,384]{1,0:T(8,128)(2,1)S(1)} %get-tuple-element.54.k_ref, bf16[3840,384]{1,0:T(8,128)(2,1)S(1)} %get-tuple-element.55.v_ref, ...), custom_call_target="tpu_custom_call" | custom-call | tf_op jit(solution)/shard_map/key_back/pallas_call | solution.py:452
  180.3 1.0 copy-done.14
  181.3 1.3 copy-done.13
  182.6 1.3 copy-done.15
  183.9 91.2 %finish.1 = (f32[768,768]{1,0:T(8,128)S(1)}, bf16[768,1536]{1,0:T(8,128)(2,1)S(1)}, f32[16,768]{1,0:T(8,128)S(1)}, bf16[768,1536]{1,0:T(8,128)(2,1)}, bf16[1536,...) custom-call(bf16[768,384]{1,0:T(8,128)(2,1)S(1)} %query_back.1.dq_ref, bf16[768,384]{1,0:T(8,128)(2,1)S(1)} %get-tuple-element.67.dk_ref, ...), custom_call_target="tpu_custom_call" | custom-call | tf_op jit(solution)/shard_map/finish/pallas_call | solution.py:1189
  275.1 1.4 copy-done.8
  276.4 1.0 copy-done.17
  278.1 0.6 slice_reduce_fusion
  278.7 0.6 reshape.160
  279.3 1.7 copy-done.6
  281.0 1.7 copy-done.7
  282.6 5.1 %widen.1 = (f32[768,384]{1,0:T(8,128)}, f32[768,384]{1,0:T(8,128)}, f32[768,384]{1,0:T(8,128)}, f32[384,768]{1,0:T(8,128)}, f32[768,1536]{1,0:T(8,128)}, /*index=5*/f32[1536,768]{1,0:T(8,128)}) custom-call(bf16[768,1536]{1,0:T(8,128)(2,1)S(1)} %get-tuple-element.80.a_ref, bf16[768,1536]{1,0:T(8,128)(2,1)S(1)} %copy-done.6, bf16[1536,768]{1,0:T(8,128)(2,1)S(1)} %copy-done.7), custom_call_target="tpu_custom_call" | custom-call | tf_op jit(solution)/shard_map/widen/pallas_call | solution.py:1233
  287.7 1.0 copy.37
  288.7 1.1 copy-done.9
  289.8 1.4 copy.38
  (43 shorter events, 1.2 us)
Async XLA Ops:
  36.7 10.5 %copy-start.10 = (bf16[768,768]{1,0:T(8,128)(2,1)}, bf16[768,768]{1,0:T(8,128)(2,1)S(1)}, u32[]{:S(2)}) copy-start(bf16[768,768]{1,0:T(8,128)(2,1)S(1)} %get-tuple-element.69.a_ref) | copy-start | bytes 3538948
  36.7 10.5 %copy-start.16 = (bf16[768,768]{1,0:T(8,128)(2,1)}, bf16[768,768]{1,0:T(8,128)(2,1)S(1)}, u32[]{:S(2)}) copy-start(bf16[768,768]{1,0:T(8,128)(2,1)S(1)} %get-tuple-element.60.wof_ref) | copy-start | bytes 3538948
  36.7 10.5 %copy-start.1 = (bf16[768,768]{1,0:T(8,128)(2,1)S(1)}, bf16[768,768]{1,0:T(8,128)(2,1)}, u32[]{:S(2)}) copy-start(bf16[768,768]{1,0:T(8,128)(2,1)} %x_ref.5) | copy-start | bytes 3538948
  148.4 16.9 %copy-start.12 = (bf16[768,768]{1,0:T(8,128)(2,1)}, bf16[768,768]{1,0:T(8,128)(2,1)S(1)}, u32[]{:S(2)}) copy-start(bf16[768,768]{1,0:T(8,128)(2,1)S(1)} %get-tuple-element.70.low_ref) | copy-start | bytes 3538948
  148.4 31.9 %collective-permute-start = (bf16[768,768]{1,0:T(8,128)(2,1)}, bf16[768,768]{1,0:T(8,128)(2,1)S(1)}, u32[]{:S(2)}, u32[]{:S(2)}) collective-permute-start(bf16[768,768]{1,0:T(8,128)(2,1)} %get-tuple-element.65.outp_hbm), channel_id=1, source_target_pairs={{0,1},{1,0},{2,3},{3,2},{4,5},{5,4},{6,7},{7,6},{8,9},{9,8},{10,11... | collective-permute-start | bytes 3538952 | tf_op jit(solution)/shard_map/ppermute | solution.py:1246
  149.9 1.8 copy-start
  165.3 16.0 %copy-start.2 = (bf16[768,768]{1,0:T(8,128)(2,1)S(1)}, bf16[768,768]{1,0:T(8,128)(2,1)}, u32[]{:S(2)}) copy-start(bf16[768,768]{1,0:T(8,128)(2,1)} %x_ref.5) | copy-start | bytes 3538948
  165.3 16.0 %copy-start.3 = (bf16[768,384]{1,0:T(8,128)(2,1)S(1)}, bf16[768,384]{1,0:T(8,128)(2,1)}, u32[]{:S(2)}) copy-start(bf16[768,384]{1,0:T(8,128)(2,1)} %wq_ref.3) | copy-start | bytes 1769476
  165.4 16.0 %copy-start.4 = (bf16[768,384]{1,0:T(8,128)(2,1)S(1)}, bf16[768,384]{1,0:T(8,128)(2,1)}, u32[]{:S(2)}) copy-start(bf16[768,384]{1,0:T(8,128)(2,1)} %wk_ref.3) | copy-start | bytes 1769476
  165.4 15.9 %copy-start.5 = (bf16[768,384]{1,0:T(8,128)(2,1)S(1)}, bf16[768,384]{1,0:T(8,128)(2,1)}, u32[]{:S(2)}) copy-start(bf16[768,384]{1,0:T(8,128)(2,1)} %wv_ref.3) | copy-start | bytes 1769476
  165.4 15.9 %copy-start.11 = (bf16[768,768]{1,0:T(8,128)(2,1)S(1)}, bf16[768,768]{1,0:T(8,128)(2,1)}, u32[]{:S(2)}) copy-start(bf16[768,768]{1,0:T(8,128)(2,1)} %copy-done.10) | copy-start | bytes 3538948
  180.3 1.0 copy-start.14
  181.3 1.3 copy-start.13
  182.6 1.3 copy-start.15
  275.0 1.4 copy-start.8
  276.4 1.0 copy-start.17
  279.3 1.7 copy-start.6
  281.0 1.7 copy-start.7
  282.6 5.1 %copy-start.18 = (bf16[768,768]{1,0:T(8,128)(2,1)S(1)}, bf16[768,768]{1,0:T(8,128)(2,1)}, u32[]{:S(2)}) copy-start(bf16[768,768]{1,0:T(8,128)(2,1)} %copy-done.17) | copy-start | bytes 3538948
  287.7 2.1 copy-start.9
where the time goes:
time: 288 us; the launch traced here: 291 us
  Pallas kernels  269 us (93%)
  local copies, waits for them, and re-layouts  16.7 us (6%)
    pallas_call x1, Pallas kernels, mid(): pl.pallas_call(mid_kernel, out_shape=(shape((blocks,) + mix.shape, BF), s...  101 us
    pallas_call x1, Pallas kernels, finish(): pl.pallas_call(functools.partial(finish_kernel, rounds), out_shape=(shape...  91.2 us
    pallas_call x3, Pallas kernels, local_call(): pl.pallas_call(kernel, grid_spec=grid, out_shape=out_shape, compiler_para...  38.9 us
    pallas_call x1, Pallas kernels, halo_qkv(): pl.pallas_call(halo_kernel, out_shape=(wide, wide, wide, shape((height, w...  33.1 us
    unnamed x40, local copies, waits for them, and re-layouts  14.7 us
  transfers between devices with their start and end apart: 1, of which 0 were waited for; matrix products, arithmetic and copies ran while one was open for 0% of the time, Pallas kernels for 10%

commit v1 on v0

--- a/solution.py
+++ b/solution.py
@@ -22,10 +22,11 @@
 F32 = jnp.float32
 MESH = pl.DeviceIdType.MESH
 VMEM = pltpu.VMEM
-VMEM_BYTES = 26_000_000
-MID_BYTES = 50_000_000
-FINISH_BYTES = 38_000_000
+VMEM_BYTES = 10_000_000
+MID_BYTES = 28_000_000
+FINISH_BYTES = 16_000_000
 PARTS = 3
+WIDEN_BYTES = 16_000_000
 STRIP = 128
 STRIPS = 3
 DMA = pltpu.SemaphoreType.DMA
@@ -187,9 +188,9 @@
             n_ref[spot, :] = jnp.maximum(n_ref[spot, :], norm)
 
     def project(slot, start):
-        spot = pl.ds(pl.multiple_of(start, half), half)
+        spot = pl.ds(pl.multiple_of(start, half // 2), half // 2)
         attn = (norm_rows(win[slot, spot, :].astype(F32)) * gain + shift).astype(BF)
-        out = pl.ds(pl.multiple_of(slot * height + start, half), half)
+        out = pl.ds(pl.multiple_of(slot * height + start, half // 2), half // 2)
 
         @pl.when(slot == REACH)
         def _():
@@ -221,66 +222,78 @@
     for copy in loads:
         copy.wait()
 
-    def half_block(i, carry):
-        @pl.when(i == 2)
+    low, high = range(PIECES // 2), range(PIECES // 2, PIECES)
+
+    def forwarded(which, pieces):
+        for side in (0, 1):
+
+            @pl.when(jnp.logical_and(exists[side], core == side))
+            def _():
+                for p in pieces:
+                    f_copy(which, p).wait_recv()
+
+    def crossed(pieces):
+        for p in pieces:
+            for side in (0, 1):
+
+                @pl.when(exists[side])
+                def _():
+                    y_copy(side, p).wait_recv()
+
+                @pl.when(jnp.logical_and(exists[side], core == 1 - side))
+                def _():
+                    f_copy(1, p).start()
+
+    def own_arrived():
+        own_copy.wait_recv()
+        w_copy.wait_recv()
+        wf_copy.start()
+
+    waits = {
+        3: [lambda: pass_on(0)],
+        4: [own_arrived],
+        6: [lambda: pass_on(1)],
+        8: [lambda: pass_on(2)] + [lambda p=p: pass_on(p) for p in range(3, PIECES // 2)],
+        10: [lambda: forwarded(0, low)],
+        11: [lambda: pass_on(high[0]), lambda: crossed(low)],
+        13: [lambda: pass_on(high[1]), lambda: forwarded(1, low)],
+        14: [lambda p=p: pass_on(p) for p in high[2:]],
+        16: [lambda: forwarded(0, high)],
+        17: [lambda: crossed(high)],
+        19: [lambda: forwarded(1, high)],
+    }
+    left, right = has_left.astype(jnp.int32), has_right.astype(jnp.int32)
+    near = (1 - core) * left + core * right
+
+    def quarter(i, carry):
+        for at, acts in waits.items():
+
+            @pl.when(i == at)
+            def _():
+                for act in acts:
+                    act()
+
+        turn = (i - 8) // 3
+        place_in = i - 8 - 3 * turn
+        late = (i >= 8).astype(jnp.int32)
+        second = (i >= 4).astype(jnp.int32)
+        first, middle = (place_in == 0).astype(jnp.int32), (place_in == 1).astype(jnp.int32)
+        third = 1 - first - middle
+        early_slot = (1 - second) * REACH + second * (3 - 2 * core)
+        late_slot = middle * 2 * REACH + third * (1 + 2 * core)
+        slot = (1 - late) * early_slot + late * late_slot
+        there = first * left + middle * right + third * near
+        odd = turn - 2 * (turn // 2)
+        late_part = 2 * ((1 - odd) * t + odd * (1 - t)) + turn // 2
+        part_of = (1 - late) * (i - 4 * second) + late * late_part
+
+        @pl.when((1 - late) + late * there == 1)
         def _():
-            pass_on(0)
-            w_copy.wait_recv()
-            wf_copy.start()
-            for p in range(1, PIECES // 2):
-                pass_on(p)
-            own_copy.wait_recv()
-
-        @pl.when(i == 4)
-        def _():
-            for p in range(PIECES // 2, PIECES):
-                pass_on(p)
-
-        @pl.when(i == 6)
-        def _():
-            for p in range(PIECES):
-                for side in (0, 1):
-
-                    @pl.when(exists[side])
-                    def _():
-                        y_copy(side, p).wait_recv()
-
-                    @pl.when(jnp.logical_and(exists[side], core == 1 - side))
-                    def _():
-                        f_copy(1, p).start()
-
-        @pl.when(i == 8)
-        def _():
-            for side in (0, 1):
-
-                @pl.when(jnp.logical_and(exists[side], core == side))
-                def _():
-                    for which in (0, 1):
-                        for p in range(PIECES):
-                            f_copy(which, p).wait_recv()
-
-        stage = i // 2
-        odd = i - 2 * stage
-        left, right = has_left.astype(jnp.int32), has_right.astype(jnp.int32)
-        near = (1 - core) * left + core * right
-        outer = (1 - odd) * left + odd * right
-
-        def pick(values):
-            total = 0
-            for index, value in enumerate(values):
-                total = total + (stage == index).astype(jnp.int32) * value
-            return total
-
-        slot = pick((REACH, 3 - 2 * core, 4 * odd, 4 * odd, 1 + 2 * core))
-        which = pick((odd, odd, t, 1 - t, odd))
-
-        @pl.when(pick((1, 1, outer, outer, near)) == 1)
-        def _():
-            project(slot, which * half)
+            project(slot, part_of * (half // 2))
 
         return carry
 
-    lax.fori_loop(0, 10, half_block, 0)
+    lax.fori_loop(0, 20, quarter, 0)
     wf_copy.wait_recv()
     for copy in (own_copy, w_copy, wf_copy):
         copy.wait_send()
@@ -856,8 +869,7 @@
             def _():
                 f_copy(p).start()
 
-    for p in range(PARTS):
-        m_copy(p).start()
+    m_copy(0).start()
     vec = row_ref[...].astype(F32)
     out_bias, gain, shift = vec[3:4], vec[4:5], vec[5:6]
     heads = pl.ds(pl.multiple_of(t * cols, cols), cols)
@@ -872,12 +884,22 @@
         dact_ref[span(p), :] = dot_nt(cot, w2_ref[...])
         vec_ref[3:4, :] += column_sums(cot.astype(F32))
         res_ref[span(p), :] = x_ref[span(p), :].astype(F32) + dot_nn(mix_ref[span(p), :], wof_ref[heads, :]) + out_bias
+
+        @pl.when(p == 0)
+        def _():
+            m_copy(1).start()
+
         return carry
 
     lax.fori_loop(0, PARTS, early, 0)
 
     def forward(p, carry):
         m_copy(p).wait_recv()
+
+        @pl.when(p == 0)
+        def _():
+            m_copy(2).start()
+
         residual = res_ref[span(p), :] + dot_nn(om_ref[span(p), :], wof_ref[others, :])
         res_ref[span(p), :] = residual
         mlp_input = (norm_rows(residual) * gain + shift).astype(BF)
@@ -1081,16 +1103,16 @@
         if s < hops - 1:
             wide.step(s)
 
+    wide.begin((own1_ref, own2_ref))
+    weights(1 - core)
+    reduce.swap(0)
     for p in range(AHEAD):
         share(p)
         y_copy(p).start()
-    wide.begin((own1_ref, own2_ref))
-    weights(1 - core)
-    reduce.swap(0)
+    weights(core)
+    wide_step(1)
     for p in range(AHEAD, PIECES):
         share(p)
-    wide_step(1)
-    weights(core)
     vec = row_ref[...].astype(F32)
     gain, fc2_bias = vec[0:1], vec[8:9]
     gains, shifts = [], []
@@ -1211,16 +1233,18 @@
     )(dq, dk, dv, wq, wk, wv, attn, low, o, x, rg, gain, vectors, own1, own2, res, outp, outo)
 
 
-def widen_kernel(a_ref, f1_ref, f2_ref, q_ref, k_ref, v_ref, o_ref, g1_ref, g2_ref):
+def widen_kernel(a_ref, f1_ref, f2_ref, i_ref, l_ref, q_ref, k_ref, v_ref, o_ref, g1_ref, g2_ref, ig_ref, lo_ref):
     cols = q_ref.shape[1]
     for i, ref in enumerate((q_ref, k_ref, v_ref)):
         ref[...] = a_ref[:, i * cols : (i + 1) * cols].astype(F32)
     o_ref[...] = jnp.transpose(a_ref[:, 3 * cols :].astype(F32))
     g1_ref[...] = f1_ref[...].astype(F32)
     g2_ref[...] = f2_ref[...].astype(F32)
-
-
-def widen(attn, f1, f2):
+    ig_ref[...] = i_ref[...]
+    lo_ref[...] = l_ref[...]
+
+
+def widen(attn, f1, f2, ig, lo):
     width = attn.shape[0]
     cols, steps = attn.shape[1] // 4, width // 128
     shape = jax.ShapeDtypeStruct
@@ -1229,17 +1253,20 @@
         return pl.BlockSpec((array.shape[0] // steps, array.shape[1]), lambda i: (i, 0))
 
     thin = shape((width, cols), F32)
-    outs = (thin, thin, thin, shape((cols, width), F32), shape(f1.shape, F32), shape(f2.shape, F32))
+    outs = (
+        thin, thin, thin, shape((cols, width), F32), shape(f1.shape, F32), shape(f2.shape, F32),
+        shape(ig.shape, ig.dtype), shape(lo.shape, lo.dtype),
+    )
     return pl.pallas_call(
         widen_kernel,
         grid=(steps,),
         out_shape=outs,
-        in_specs=[block(attn), block(f1), block(f2)],
+        in_specs=[block(attn), block(f1), block(f2), block(ig), block(lo)],
         out_specs=[block(thin)] * 3
-        + [pl.BlockSpec((cols, 128), lambda i: (0, i)), block(f1), block(f2)],
-        compiler_params=pltpu.CompilerParams(vmem_limit_bytes=VMEM_BYTES),
+        + [pl.BlockSpec((cols, 128), lambda i: (0, i)), block(f1), block(f2), block(ig), block(lo)],
+        compiler_params=pltpu.CompilerParams(vmem_limit_bytes=WIDEN_BYTES),
         name="widen",
-    )(attn, f1, f2)
+    )(attn, f1, f2, ig, lo)
 
 
 def swapped(value):
@@ -1289,7 +1316,10 @@
         query_low, key_low, value_low, w_query, w_key, w_value, attn_input, low, mixed, inputs,
         residual_grad, vec, vectors, own1, own2, residual, out_part, out_other, (w_fc1.shape, w_fc2.shape),
     )
-    q_grad, k_grad, v_grad, o_grad, fc1_grad, fc2_grad = widen(attn_sum, fc1_sum, fc2_sum)
+    q_grad, k_grad, v_grad, o_grad, fc1_grad, fc2_grad, inputs_grad, layer_out = widen(
+        attn_sum, fc1_sum, fc2_sum, inputs_grad, layer_out
+    )
+    sums, q_grad = lax.optimization_barrier((sums, q_grad))
     return (
         layer_out, inputs_grad, sums[7], sums[8],
         q_grad, sums[6, :cols], k_grad, v_grad, sums[6, cols:],

time: 288 us -> 258 us (0.90)
  Pallas kernels: 269 us -> 250 us
  local copies, waits for them, and re-layouts: 16.7 us -> 2.08 us
    unnamed x40 -> x14, local copies, waits for them, and re-layouts: 14.7 us -> 0.04 us
    pallas_call x1, Pallas kernels: 101 us -> 91.8 us  [mid(): pl.pallas_call(mid_kernel, out_shape=(shape((blocks,) + mix.shape, BF), s...]
    pallas_call x1, Pallas kernels: 91.2 us -> 82.2 us  [finish(): pl.pallas_call(functools.partial(finish_kernel, rounds), out_shape=(shape...]
  transfers between devices with their start and end apart: 1 -> 1, of which waited for: 0 -> 1; matrix products, arithmetic and copies ran while one was open for 0% -> 0% of each run, Pallas kernels for 10% -> 9%
where the time goes in v1:
time: 258 us; the launch traced here: 262 us
  Pallas kernels  250 us (97%)
  starting transfers between devices  3.7 us (1%)
  other arithmetic  2.74 us (1%)
    pallas_call x1, Pallas kernels, mid(): pl.pallas_call(mid_kernel, out_shape=(shape((blocks,) + mix.shape, BF), s...  91.8 us
    pallas_call x1, Pallas kernels, finish(): pl.pallas_call(functools.partial(finish_kernel, rounds), out_shape=(shape...  82.2 us
    pallas_call x3, Pallas kernels, local_call(): pl.pallas_call(kernel, grid_spec=grid, out_shape=out_shape, compiler_para...  37.2 us
    pallas_call x1, Pallas kernels, halo_qkv(): pl.pallas_call(halo_kernel, out_shape=(wide, wide, wide, shape((height, w...  33 us
    pallas_call x1, Pallas kernels, widen(): pl.pallas_call(widen_kernel, grid=(steps,), out_shape=outs, in_specs=[blo...  6.17 us
  transfers between devices with their start and end apart: 1, of which 1 were waited for; matrix products, arithmetic and copies ran while one was open for 0% of the time, Pallas kernels for 9%

profile of v1, /device:TPU:0, one launch (start us, length us, event | category | flops | bytes accessed | tf_op | source)
XLA Modules:
  0.0 261.7 jit_solution(15362219132486766380)
XLA Ops:
  0.7 0.8 convert_bitcast_fusion
  1.5 0.1 slice.44
  1.6 0.1 slice.43
  1.7 0.2 convert_reduce_fusion.1
  2.0 0.8 fusion.2
  2.8 0.9 select_select_fusion.vec_ref.row_ref
  3.6 33.0 %halo_qkv.1 = (bf16[3840,384]{1,0:T(8,128)(2,1)S(1)}, bf16[3840,384]{1,0:T(8,128)(2,1)S(1)}, bf16[3840,384]{1,0:T(8,128)(2,1)S(1)}, bf16[768,768]{1,0:T(8,128)(2...) custom-call(bf16[768,768]{1,0:T(8,128)(2,1)} %x_ref.5, ...), custom_call_target="tpu_custom_call" | custom-call | tf_op jit(solution)/shard_map/halo_qkv/pallas_call | solution.py:324
  36.7 0.0 copy-start
  36.7 0.0 copy-start.4
  36.7 0.0 copy-start.5
  36.7 0.0 copy-start.6
  36.7 13.9 %attend.1 = (bf16[768,384]{1,0:T(8,128)(2,1)S(1)}, f32[8,768]{1,0:T(8,128)S(1)}) custom-call(s32[2,3]{1,0:T(2,128)S(1)} %pad_add_fusion.1.b_ref, bf16[3840,384]{1,0:T(8,128)(2,1)S(1)} %get-tuple-element.57.q_ref, bf16[3840,384]{1,0:T(8,128)(2,1)S(1)} %get-tuple-element.58.k_ref, bf16[3840,384]{1,0:T(8,128)(2,1)S(1)} %get-tuple-element.59.v_ref, ...), custom_call_target="tpu_custom_call" | custom-call | tf_op jit(solution)/shard_map/attend/pallas_call | solution.py:465
  50.7 91.8 %mid.1 = (bf16[5,768,384]{2,1,0:T(8,128)(2,1)S(1)}, bf16[3840,128]{1,0:T(8,128)(2,1)S(1)}, f32[768,768]{1,0:T(8,128)S(1)}, bf16[768,768]{1,0:T(8,128)(2,1)S(1)},...) custom-call(bf16[768,768]{1,0:T(8,128)(2,1)S(1)} %copy-done, ...), custom_call_target="tpu_custom_call" | custom-call | tf_op jit(solution)/shard_map/mid/pallas_call | solution.py:1029
  142.5 3.7 %collective-permute-start = (bf16[768,768]{1,0:T(8,128)(2,1)S(1)}, bf16[768,768]{1,0:T(8,128)(2,1)S(1)}, u32[]{:S(2)}, u32[]{:S(2)}) collective-permute-start(bf16[768,768]{1,0:T(8,128)(2,1)S(1)} %get-tuple-element.69.outp_hbm), channel_id=1, source_target_pairs={{0,1},{1,0},{2,3},{3,2},{4,5},{5,4},{6,7},{7,6},{8,9},{9,8},{10,11... | collective-permute-start | bytes 3538952 | tf_op jit(solution)/shard_map/ppermute | solution.py:1273
  146.2 11.2 %query_back.1.dq_ref = bf16[768,384]{1,0:T(8,128)(2,1)S(1)} custom-call(s32[2,3]{1,0:T(2,128)S(1)} %pad_add_fusion.1.b_ref, bf16[3840,384]{1,0:T(8,128)(2,1)S(1)} %get-tuple-element.57.q_ref, bf16[3840,384]{1,0:T(8,128)(2,1)S(1)} %get-tuple-element.58.k_ref, bf16[3840,384]{1,0:T(8,128)(2,1)S(1)} %get-tuple-element.59.v_ref, bf16[3840,384]{1,0:T(8,128)(2,1)S(1)} %bitcast.19, ...), custom_call_target="tpu_custom_call" | custom-call | tf_op jit(solution)/shard_map/query_back/pallas_call | solution.py:465
  157.4 0.0 copy-start.1
  157.4 0.0 copy-start.3
  157.4 12.1 %key_back.1 = (bf16[768,384]{1,0:T(8,128)(2,1)S(1)}, bf16[768,384]{1,0:T(8,128)(2,1)S(1)}) custom-call(s32[2,3]{1,0:T(2,128)S(1)} %pad_add_fusion.1.b_ref, bf16[3840,384]{1,0:T(8,128)(2,1)S(1)} %get-tuple-element.57.q_ref, bf16[3840,384]{1,0:T(8,128)(2,1)S(1)} %get-tuple-element.58.k_ref, bf16[3840,384]{1,0:T(8,128)(2,1)S(1)} %get-tuple-element.59.v_ref, ...), custom_call_target="tpu_custom_call" | custom-call | tf_op jit(solution)/shard_map/key_back/pallas_call | solution.py:465
  169.5 1.9 collective-permute-done.outo_hbm
  171.4 82.2 %finish.1 = (f32[768,768]{1,0:T(8,128)S(1)}, bf16[768,1536]{1,0:T(8,128)(2,1)S(1)}, f32[16,768]{1,0:T(8,128)S(1)}, bf16[768,1536]{1,0:T(8,128)(2,1)S(1)}, bf16[1...) custom-call(bf16[768,384]{1,0:T(8,128)(2,1)S(1)} %query_back.1.dq_ref, ...), custom_call_target="tpu_custom_call" | custom-call | tf_op jit(solution)/shard_map/finish/pallas_call | solution.py:1211
  253.7 6.2 %widen.1 = (f32[768,384]{1,0:T(8,128)}, f32[768,384]{1,0:T(8,128)}, f32[768,384]{1,0:T(8,128)}, f32[384,768]{1,0:T(8,128)}, f32[768,1536]{1,0:T(8,128)}, /*index...) custom-call(bf16[768,1536]{1,0:T(8,128)(2,1)S(1)} %get-tuple-element.81.a_ref, ...), custom_call_target="tpu_custom_call" | custom-call | tf_op jit(solution)/shard_map/widen/pallas_call | solution.py:1260
  259.8 0.6 slice_reduce_fusion.6
  260.4 0.6 slice_reduce_fusion
  261.1 0.6 reshape.160
  (17 shorter events, 0.1 us)
Async XLA Ops:
  36.7 13.9 %copy-start = (bf16[768,768]{1,0:T(8,128)(2,1)S(1)}, bf16[768,768]{1,0:T(8,128)(2,1)}, u32[]{:S(2)}) copy-start(bf16[768,768]{1,0:T(8,128)(2,1)} %x_ref.5) | copy-start | bytes 3538948
  36.7 13.9 %copy-start.4 = (bf16[768,1536]{1,0:T(8,128)(2,1)S(1)}, bf16[768,1536]{1,0:T(8,128)(2,1)}, u32[]{:S(2)}) copy-start(bf16[768,1536]{1,0:T(8,128)(2,1)} %w1_ref.1) | copy-start | bytes 7077892
  36.7 13.9 %copy-start.5 = (bf16[1536,768]{1,0:T(8,128)(2,1)S(1)}, bf16[1536,768]{1,0:T(8,128)(2,1)}, u32[]{:S(2)}) copy-start(bf16[1536,768]{1,0:T(8,128)(2,1)} %w2_ref.1) | copy-start | bytes 7077892
  36.7 13.9 %copy-start.6 = (bf16[768,768]{1,0:T(8,128)(2,1)S(1)}, bf16[768,768]{1,0:T(8,128)(2,1)}, u32[]{:S(2)}) copy-start(bf16[768,768]{1,0:T(8,128)(2,1)} %cot_ref.1) | copy-start | bytes 3538948
  142.5 28.9 %collective-permute-start = (bf16[768,768]{1,0:T(8,128)(2,1)S(1)}, bf16[768,768]{1,0:T(8,128)(2,1)S(1)}, u32[]{:S(2)}, u32[]{:S(2)}) collective-permute-start(bf16[768,768]{1,0:T(8,128)(2,1)S(1)} %get-tuple-element.69.outp_hbm), channel_id=1, source_target_pairs={{0,1},{1,0},{2,3},{3,2},{4,5},{5,4},{6,7},{7,6},{8,9},{9,8},{10,11... | collective-permute-start | bytes 3538952 | tf_op jit(solution)/shard_map/ppermute | solution.py:1273
  157.4 14.0 %copy-start.1 = (bf16[768,384]{1,0:T(8,128)(2,1)S(1)}, bf16[768,384]{1,0:T(8,128)(2,1)}, u32[]{:S(2)}) copy-start(bf16[768,384]{1,0:T(8,128)(2,1)} %wq_ref.3) | copy-start | bytes 1769476
  157.4 14.0 %copy-start.2 = (bf16[768,384]{1,0:T(8,128)(2,1)S(1)}, bf16[768,384]{1,0:T(8,128)(2,1)}, u32[]{:S(2)}) copy-start(bf16[768,384]{1,0:T(8,128)(2,1)} %wk_ref.3) | copy-start | bytes 1769476
  157.4 14.0 %copy-start.3 = (bf16[768,384]{1,0:T(8,128)(2,1)S(1)}, bf16[768,384]{1,0:T(8,128)(2,1)}, u32[]{:S(2)}) copy-start(bf16[768,384]{1,0:T(8,128)(2,1)} %wv_ref.3) | copy-start | bytes 1769476

commit v2 on v1

--- a/solution.py
+++ b/solution.py
@@ -13,9 +13,9 @@
 PIECES = 6
 AHEAD = 2
 NEG = -3e38
-CLIPS = 64
-LOGS = 64
-CENTRES = 96
+CLIPS = 49
+LOGS = 49
+CENTRES = 52
 FAR = -(2.0**100)
 SAFE = 40.0
 BF = jnp.bfloat16
@@ -175,6 +175,7 @@
     def code(r, carry):
         labels = jnp.transpose(jnp.broadcast_to(lab_ref[pl.ds(r, 1), :], (128, 128)))
         lane = lax.broadcasted_iota(jnp.int32, (128, 128), 1)
+        lane = lane - HEAD_DIM * (lane // HEAD_DIM)
         far = jnp.where(labels == lane.astype(F32), 0.0, FAR)
         kc_ref[pl.ds(pl.multiple_of(r * 128, 128), 128), :] = jnp.where(lane < CLIPS, far, 1.0).astype(BF)
         return carry
@@ -345,19 +346,29 @@
     return first, second, values - first - second
 
 
-def code_tile(rows, keys_code):
-    count = rows.shape[1]
-    terms = split3(-rows)
-    lane = lax.broadcasted_iota(jnp.int32, (128, count), 0)
-    tall = jnp.zeros((128, count), F32)
-    for h in range(8):
-        for base, row in ((LOGS, h), (CENTRES, 8 + h)):
-            for i in range(3):
-                tall = jnp.where(lane == base + 3 * h + i, terms[i][row : row + 1], tall)
-    wide = jnp.transpose(tall)
-    column = lax.broadcasted_iota(jnp.int32, wide.shape, 1)
-    same = jnp.logical_and(column < CLIPS, keys_code.astype(F32) == 0.0)
-    return jnp.where(same, 1.0, wide).astype(BF)
+def free_lane(shape):
+    lane = lax.broadcasted_iota(jnp.int32, shape, 1)
+    return lane - HEAD_DIM * (lane // HEAD_DIM)
+
+
+def clip_code(keys_code):
+    same = jnp.logical_and(free_lane(keys_code.shape) < CLIPS, keys_code.astype(F32) == 0.0)
+    return jnp.where(same, 1.0, 0.0)
+
+
+def code_tile(rows, keys_code, cols):
+    terms = jnp.concatenate(split3(-rows), axis=0).astype(BF)
+    line = lax.broadcasted_iota(jnp.int32, (48, cols), 0)
+    lane = lax.broadcasted_iota(jnp.int32, (48, cols), 1)
+    term = line // 16
+    row = line - 16 * term
+    centre = row // 8
+    head = row - 8 * centre
+    pair = head // 2
+    spot = 128 * pair + HEAD_DIM * (1 - (head - 2 * pair)) + LOGS + (CENTRES - LOGS) * centre + term
+    picks = jnp.where(lane == spot, 1.0, 0.0).astype(BF)
+    same = clip_code(keys_code)
+    return (dot_tn(terms, picks) + jnp.concatenate([same] * (cols // 128), axis=1)).astype(BF)
 
 
 def tile_at(j):
@@ -368,50 +379,45 @@
     return pl.ds(c * 128, 128)
 
 
-def beside(left, right):
-    return jnp.concatenate([left, right], axis=1)
-
-
-def stacked_heads(values, codes):
+def with_code(values, code):
     lower = lax.broadcasted_iota(jnp.int32, values.shape, 1) < HEAD_DIM
-    none = jnp.zeros_like(values)
-    return jnp.concatenate(
-        [beside(jnp.where(lower, values, none), codes[0]), beside(jnp.where(lower, none, values), codes[1])],
-        axis=0,
-    )
-
-
-def heads_out(turned):
-    pair = jnp.concatenate([turned[:HEAD_DIM, :TILE], turned[HEAD_DIM:, TILE:]], axis=0)
-    return jnp.transpose(pair)
-
-
-def within(lane, start):
-    return jnp.logical_and(lane >= start, lane < start + 3)
-
-
-def attfinish_kernel(b_ref, q_ref, k_ref, v_ref, kc_ref, n_ref, o_ref, lse_ref, r_ref, m_ref, l_ref, acc_ref):
-    height, cols = o_ref.shape
-    pairs, tiles = cols // 128, height // TILE
+    return jnp.where(lower, values, code), jnp.where(lower, code, values)
+
+
+def against(moving, still):
+    return jnp.concatenate([dot_nt(moving[h], still[h * TILE : (h + 1) * TILE]) for h in (0, 1)], axis=1)
+
+
+def add_heads(acc_ref, c, values, weights):
+    turned = jnp.transpose(values)
+    acc_ref[c, :HEAD_DIM] += dot_nn(turned[:HEAD_DIM], weights[:, :TILE])
+    acc_ref[c, HEAD_DIM:] += dot_nn(turned[HEAD_DIM:], weights[:, TILE:])
+
+
+def keep(code, low, high):
+    lane = free_lane(code.shape)
+    return jnp.where(jnp.logical_and(lane >= low, lane < high), code, jnp.zeros_like(code))
+
+
+def attend_kernel(height, first, b_ref, q_ref, k_ref, v_ref, kc_ref, n_ref, o_ref, lse_ref, r_ref, m_ref, l_ref, acc_ref):
+    cols = o_ref.shape[1]
+    pairs, tiles = cols // 128, o_ref.shape[0] // TILE
     steep = jnp.logical_not(jnp.max(n_ref[0:8, :]) * jnp.max(n_ref[8:16, :]) <= SAFE * SAFE)
-    lane = lax.broadcasted_iota(jnp.int32, (TILE, 128), 1)
-
     def groups(values):
         return values.reshape(TILE // 8, 8, values.shape[1])
 
     def one(i, carry):
-        lo, hi = b_ref[0, i], b_ref[1, i]
-        own = pl.ds(pl.multiple_of(REACH * height + i * TILE, TILE), TILE)
-        same = jnp.logical_and(lane < CLIPS, kc_ref[own, :].astype(F32) == 0.0)
-        code = jnp.where(same, 1.0, 0.0).astype(BF)
+        lo, hi = b_ref[0, first + i], b_ref[1, first + i]
+        own = pl.ds(pl.multiple_of(REACH * height + (first + i) * TILE, TILE), TILE)
+        code = clip_code(kc_ref[own, :]).astype(BF)
         for c in range(pairs):
-            r_ref[c] = stacked_heads(q_ref[own, lanes_of(c)], (code, code))
+            r_ref[c] = jnp.concatenate(with_code(q_ref[own, lanes_of(c)], code), axis=0)
         acc_ref[...] = jnp.zeros(acc_ref.shape, F32)
         l_ref[...] = jnp.zeros(l_ref.shape, F32)
         m_ref[...] = jnp.zeros(m_ref.shape, F32)
 
         def score(j, c):
-            return dot_nt(beside(k_ref[tile_at(j), lanes_of(c)], kc_ref[tile_at(j), :]), r_ref[c])
+            return against(with_code(k_ref[tile_at(j), lanes_of(c)], kc_ref[tile_at(j), :]), r_ref[c])
 
         def step(shift, j, carry):
             raised = []
@@ -421,7 +427,7 @@
                 l_ref[c] += jnp.sum(groups(e), axis=0)
                 raised.append(e.astype(BF))
             for c in range(pairs):
-                acc_ref[c] += dot_tn(v_ref[tile_at(j), lanes_of(c)], raised[c])
+                add_heads(acc_ref, c, v_ref[tile_at(j), lanes_of(c)], raised[c])
             return carry
 
         @pl.when(jnp.logical_not(steep))
@@ -444,7 +450,10 @@
 
         for c in range(pairs):
             total = jnp.sum(l_ref[c], axis=0, keepdims=True)
-            o_ref[tile_at(i), lanes_of(c)] = heads_out(acc_ref[c] / total).astype(BF)
+            share = jnp.concatenate(
+                [acc_ref[c, :HEAD_DIM] / total[:, :TILE], acc_ref[c, HEAD_DIM:] / total[:, TILE:]], axis=0
+            )
+            o_ref[tile_at(i), lanes_of(c)] = jnp.transpose(share).astype(BF)
             logs = m_ref[c, 0:1, :] + jnp.log(total)
             lse_ref[2 * c : 2 * c + 1, tile_at(i)] = logs[:, :TILE]
             lse_ref[2 * c + 1 : 2 * c + 2, tile_at(i)] = logs[:, TILE:]
@@ -471,51 +480,47 @@
     )(bounds, *values)
 
 
-def attend(bounds, q, k, v, kc, norms, height):
+def attend(bounds, q, k, v, kc, norms, height, first, count):
     cols = k.shape[1]
     pairs = cols // 128
-    out_shape = (jax.ShapeDtypeStruct((height, cols), BF), jax.ShapeDtypeStruct((8, height), F32))
+    rows = count * TILE
+    out_shape = (jax.ShapeDtypeStruct((rows, cols), BF), jax.ShapeDtypeStruct((8, rows), F32))
     scratch = [
-        pltpu.VMEM((pairs, 2 * TILE, 256), BF),
+        pltpu.VMEM((pairs, 2 * TILE, 128), BF),
         pltpu.VMEM((pairs, 8, 2 * TILE), F32),
         pltpu.VMEM((pairs, 8, 2 * TILE), F32),
-        pltpu.VMEM((pairs, 128, 2 * TILE), F32),
+        pltpu.VMEM((pairs, 128, TILE), F32),
     ]
-    return local_call(attfinish_kernel, "attend", out_shape, scratch, bounds, q, k, v, kc, norms)
+    kernel = functools.partial(attend_kernel, height, first)
+    return local_call(kernel, "attend", out_shape, scratch, bounds, q, k, v, kc, norms)
 
 
 def query_back_kernel(b_ref, q_ref, k_ref, v_ref, g_ref, kc_ref, qc_ref, dq_ref, r_ref, t_ref, acc_ref):
     height, cols = dq_ref.shape
     pairs, tiles = cols // 128, height // TILE
-    lane = lax.broadcasted_iota(jnp.int32, (TILE, 128), 1)
-
     def one(i, carry):
         own = pl.ds(pl.multiple_of(REACH * height + i * TILE, TILE), TILE)
-        code = qc_ref[own, :]
-        none = jnp.zeros_like(code)
         for c in range(pairs):
-            logs, centres = [], []
-            for h in (2 * c, 2 * c + 1):
-                logs.append(jnp.where(jnp.logical_or(lane < CLIPS, within(lane, LOGS + 3 * h)), code, none))
-                centres.append(jnp.where(within(lane, CENTRES + 3 * h), code, none))
-            r_ref[c] = stacked_heads(q_ref[own, lanes_of(c)], logs)
-            t_ref[c] = stacked_heads(g_ref[own, lanes_of(c)], centres)
+            code = qc_ref[own, lanes_of(c)]
+            logs, centres = keep(code, 0, CENTRES), keep(code, CENTRES, CENTRES + 3)
+            r_ref[c] = jnp.concatenate(with_code(q_ref[own, lanes_of(c)], logs), axis=0)
+            t_ref[c] = jnp.concatenate(with_code(g_ref[own, lanes_of(c)], centres), axis=0)
         acc_ref[...] = jnp.zeros(acc_ref.shape, F32)
 
         def step(j, carry):
             code = kc_ref[tile_at(j), :]
             steps = []
             for c in range(pairs):
-                probs = jnp.exp(dot_nt(beside(k_ref[tile_at(j), lanes_of(c)], code), r_ref[c]))
-                d_probs = dot_nt(beside(v_ref[tile_at(j), lanes_of(c)], code), t_ref[c])
+                probs = jnp.exp(against(with_code(k_ref[tile_at(j), lanes_of(c)], code), r_ref[c]))
+                d_probs = against(with_code(v_ref[tile_at(j), lanes_of(c)], code), t_ref[c])
                 steps.append((probs * d_probs).astype(BF))
             for c in range(pairs):
-                acc_ref[c] += dot_tn(k_ref[tile_at(j), lanes_of(c)], steps[c])
+                add_heads(acc_ref, c, k_ref[tile_at(j), lanes_of(c)], steps[c])
             return carry
 
         lax.fori_loop(b_ref[0, i], b_ref[1, i], step, 0)
         for c in range(pairs):
-            dq_ref[tile_at(i), lanes_of(c)] = (heads_out(acc_ref[c]) * HEAD_DIM**-0.5).astype(BF)
+            dq_ref[tile_at(i), lanes_of(c)] = (jnp.transpose(acc_ref[c]) * HEAD_DIM**-0.5).astype(BF)
         return carry
 
     lax.fori_loop(0, tiles, one, 0)
@@ -524,7 +529,7 @@
 def query_back(bounds, q, k, v, g, kc, qc, height):
     cols = k.shape[1]
     pairs = cols // 128
-    scratch = [pltpu.VMEM((pairs, 2 * TILE, 256), BF)] * 2 + [pltpu.VMEM((pairs, 128, 2 * TILE), F32)]
+    scratch = [pltpu.VMEM((pairs, 2 * TILE, 128), BF)] * 2 + [pltpu.VMEM((pairs, 128, TILE), F32)]
     out_shape = jax.ShapeDtypeStruct((height, cols), BF)
     return local_call(query_back_kernel, "query_back", out_shape, scratch, bounds, q, k, v, g, kc, qc)
 
@@ -532,39 +537,33 @@
 def key_back_kernel(b_ref, q_ref, k_ref, v_ref, g_ref, kc_ref, qc_ref, dk_ref, dv_ref, r_ref, t_ref, ak_ref, av_ref):
     height, cols = dk_ref.shape
     pairs, tiles = cols // 128, height // TILE
-    lane = lax.broadcasted_iota(jnp.int32, (TILE, 128), 1)
-
     def one(i, carry):
         own = pl.ds(pl.multiple_of(REACH * height + i * TILE, TILE), TILE)
         code = kc_ref[own, :]
-        none, ones = jnp.zeros_like(code), jnp.ones_like(code)
+        logs, centres = keep(code, 0, CENTRES), keep(code, CENTRES, CENTRES + 3)
         for c in range(pairs):
-            logs, centres = [], []
-            for h in (2 * c, 2 * c + 1):
-                logs.append(jnp.where(lane < CLIPS, code, jnp.where(within(lane, LOGS + 3 * h), ones, none)))
-                centres.append(jnp.where(within(lane, CENTRES + 3 * h), ones, none))
-            r_ref[c] = stacked_heads(k_ref[own, lanes_of(c)], logs)
-            t_ref[c] = stacked_heads(v_ref[own, lanes_of(c)], centres)
+            r_ref[c] = jnp.concatenate(with_code(k_ref[own, lanes_of(c)], logs), axis=0)
+            t_ref[c] = jnp.concatenate(with_code(v_ref[own, lanes_of(c)], centres), axis=0)
         ak_ref[...] = jnp.zeros(ak_ref.shape, F32)
         av_ref[...] = jnp.zeros(av_ref.shape, F32)
 
         def step(j, carry):
-            code = qc_ref[tile_at(j), :]
             weights, steps = [], []
             for c in range(pairs):
-                probs = jnp.exp(dot_nt(beside(q_ref[tile_at(j), lanes_of(c)], code), r_ref[c]))
-                d_probs = dot_nt(beside(g_ref[tile_at(j), lanes_of(c)], code), t_ref[c])
+                code = qc_ref[tile_at(j), lanes_of(c)]
+                probs = jnp.exp(against(with_code(q_ref[tile_at(j), lanes_of(c)], code), r_ref[c]))
+                d_probs = against(with_code(g_ref[tile_at(j), lanes_of(c)], code), t_ref[c])
                 weights.append(probs.astype(BF))
                 steps.append((probs * d_probs).astype(BF))
             for c in range(pairs):
-                av_ref[c] += dot_tn(g_ref[tile_at(j), lanes_of(c)], weights[c])
-                ak_ref[c] += dot_tn(q_ref[tile_at(j), lanes_of(c)], steps[c])
+                add_heads(av_ref, c, g_ref[tile_at(j), lanes_of(c)], weights[c])
+                add_heads(ak_ref, c, q_ref[tile_at(j), lanes_of(c)], steps[c])
             return carry
 
         lax.fori_loop(b_ref[0, i], b_ref[1, i], step, 0)
         for c in range(pairs):
-            dk_ref[tile_at(i), lanes_of(c)] = heads_out(ak_ref[c]).astype(BF)
-            dv_ref[tile_at(i), lanes_of(c)] = heads_out(av_ref[c]).astype(BF)
+            dk_ref[tile_at(i), lanes_of(c)] = jnp.transpose(ak_ref[c]).astype(BF)
+            dv_ref[tile_at(i), lanes_of(c)] = jnp.transpose(av_ref[c]).astype(BF)
         return carry
 
     lax.fori_loop(0, tiles, one, 0)
@@ -573,7 +572,7 @@
 def key_back(bounds, q, k, v, g, kc, qc, height):
     cols = k.shape[1]
     pairs = cols // 128
-    scratch = [pltpu.VMEM((pairs, 2 * TILE, 256), BF)] * 2 + [pltpu.VMEM((pairs, 128, 2 * TILE), F32)] * 2
+    scratch = [pltpu.VMEM((pairs, 2 * TILE, 128), BF)] * 2 + [pltpu.VMEM((pairs, 128, TILE), F32)] * 2
     out_shape = (jax.ShapeDtypeStruct((height, cols), BF),) * 2
     return local_call(key_back_kernel, "key_back", out_shape, scratch, bounds, q, k, v, g, kc, qc)
 
@@ -797,8 +796,8 @@
 
 
 def mid_kernel(
-    x_ref, cot_ref, mix_ref, lse_ref, kc_ref, wof_ref, row_ref, w1_ref, w2_ref,
-    xw_ref, qc_ref, rg_ref, low_ref, vec_ref, own1_ref, own2_ref, res_ref, outp_ref,
+    x_ref, cot_ref, mixa_ref, mixb_ref, oma_ref, lsea_ref, lseb_ref, kc_ref, wof_ref, row_ref, w1_ref, w2_ref,
+    xw_ref, qc_ref, rg_ref, low_ref, vec_ref, own1_ref, own2_ref, res_ref, outp_ref, mix_ref,
     om_ref, dact_ref, mi_ref, act_ref, pg_ref, part_ref, oth_ref, f1_ref, f2_ref, st_ref, sw_ref,
     sib1, sib2, buf1, buf2,
     sm, rm, sy, ry, sx, rx, ss, rs, sf, rf, *ring_sems,
@@ -823,8 +822,8 @@
     def span(p):
         return pl.ds(pl.multiple_of(p * rows, rows), rows)
 
-    def m_copy(p):
-        return remote(mix_ref.at[span(p)], om_ref.at[span(p)], sm.at[p], rm.at[p], across)
+    head = mixa_ref.shape[0]
+    m_copy = remote(mixb_ref, om_ref.at[pl.ds(head, height - head)], sm, rm, across)
 
     def y_copy(p):
         return remote(part_ref.at[span(p)], oth_ref.at[span(p)], sy.at[p], ry.at[p], across)
@@ -869,14 +868,18 @@
             def _():
                 f_copy(p).start()
 
-    m_copy(0).start()
+    m_copy.start()
+    mix_ref[:head, :] = mixa_ref[...]
+    mix_ref[head:, :] = mixb_ref[...]
+    om_ref[:head, :] = oma_ref[...]
     vec = row_ref[...].astype(F32)
     out_bias, gain, shift = vec[3:4], vec[4:5], vec[5:6]
     heads = pl.ds(pl.multiple_of(t * cols, cols), cols)
     others = pl.ds(pl.multiple_of((1 - t) * cols, cols), cols)
     picks = lax.broadcasted_iota(jnp.int32, (8, cols), 1) // HEAD_DIM
     picks = (picks == lax.broadcasted_iota(jnp.int32, (8, cols), 0)).astype(F32)
-    st_ref[0:8, :] = lse_ref[...]
+    st_ref[0:8, :head] = lsea_ref[...]
+    st_ref[0:8, head:] = lseb_ref[...]
     vec_ref[...] = jnp.zeros(vec_ref.shape, F32)
 
     def early(p, carry):
@@ -884,21 +887,14 @@
         dact_ref[span(p), :] = dot_nt(cot, w2_ref[...])
         vec_ref[3:4, :] += column_sums(cot.astype(F32))
         res_ref[span(p), :] = x_ref[span(p), :].astype(F32) + dot_nn(mix_ref[span(p), :], wof_ref[heads, :]) + out_bias
-
-        @pl.when(p == 0)
+        return carry
+
+    lax.fori_loop(0, PARTS, early, 0)
+
+    def forward(p, carry):
+        @pl.when((p + 1) * rows > head)
         def _():
-            m_copy(1).start()
-
-        return carry
-
-    lax.fori_loop(0, PARTS, early, 0)
-
-    def forward(p, carry):
-        m_copy(p).wait_recv()
-
-        @pl.when(p == 0)
-        def _():
-            m_copy(2).start()
+            m_copy.wait_recv()
 
         residual = res_ref[span(p), :] + dot_nn(om_ref[span(p), :], wof_ref[others, :])
         res_ref[span(p), :] = residual
@@ -948,7 +944,7 @@
         def step(i, carry):
             spot = pl.ds(pl.multiple_of(slot * height + i * TILE, TILE), TILE)
             stats = sw_ref[slot, :, pl.ds(pl.multiple_of(i * TILE, TILE), TILE)]
-            qc_ref[spot, :] = code_tile(stats, kc_ref[spot, :])
+            qc_ref[spot, :] = code_tile(stats, kc_ref[spot, :], cols)
             return carry
 
         lax.fori_loop(0, height // TILE, step, 0)
@@ -967,13 +963,13 @@
     weights(core)
     reduce.first(0)
     reduce.first(1)
+    outp_ref[...] = dot_nn(act_ref[...], w2_ref[...]).astype(BF)
+    ring_step(1)
     back(2)
     send(2)
     send(PARTS)
     sw_ref[REACH] = st_ref[...]
-    ring_step(1)
     pass_on(0)
-    outp_ref[...] = dot_nn(act_ref[...], w2_ref[...]).astype(BF)
     ring_step(2)
     pass_on(1)
     between(reduce.step, 3, hops)
@@ -1012,15 +1008,16 @@
             code(1 + 2 * core)
 
     for p in range(PARTS):
-        m_copy(p).wait_send()
         y_copy(p).wait_send()
+    m_copy.wait_send()
     reduce.settle()
 
 
-def mid(x, cot, mix, lse, kc, wof, vec, w1, w2):
+def mid(x, cot, mixa, mixb, oma, lsea, lseb, kc, wof, vec, w1, w2):
     blocks = 2 * REACH + 1
     height, width = x.shape
     hidden = w1.shape[1]
+    mix = jax.ShapeDtypeStruct((height, mixa.shape[1]), BF)
     n = lax.axis_size("dp") // 2
     pair, line, some = DMA((2, PARTS + 1)), DMA((PARTS + 1,)), DMA((PARTS,))
     room, sems = reduce_scratch((w1.shape, w2.shape), n)
@@ -1029,11 +1026,11 @@
     return pl.pallas_call(
         mid_kernel,
         out_shape=(
-            shape((blocks,) + mix.shape, BF), shape(kc.shape, BF), shape(x.shape, F32), shape(x.shape, BF),
-            shape((16, width), F32), *chunks, shape(x.shape, F32), shape(x.shape, BF),
+            shape((blocks,) + mix.shape, BF), shape((kc.shape[0], mix.shape[1]), BF), shape(x.shape, F32), shape(x.shape, BF),
+            shape((16, width), F32), *chunks, shape(x.shape, F32), shape(x.shape, BF), mix,
         ),
-        in_specs=[whole()] * 9,
-        out_specs=[whole()] * 9,
+        in_specs=[whole()] * 12,
+        out_specs=[whole()] * 10,
         scratch_shapes=[
             pltpu.VMEM(mix.shape, BF), pltpu.VMEM((height, hidden), F32), pltpu.VMEM(x.shape, BF),
             pltpu.VMEM((height, hidden), BF), pltpu.VMEM((height, hidden), BF), pltpu.VMEM(x.shape, BF),
@@ -1041,13 +1038,13 @@
             pltpu.VMEM((16, height), F32), pltpu.VMEM((blocks, 16, height), F32),
         ]
         + room
-        + [some, some, some, some, pair, pair, line, line, line, line]
+        + [DMA, DMA, some, some, pair, pair, line, line, line, line]
         + sems,
         compiler_params=pltpu.CompilerParams(
             collective_id=1, has_side_effects=True, vmem_limit_bytes=MID_BYTES
         ),
         name="mid",
-    )(x, cot, mix, lse, kc, wof, vec, w1, w2)
+    )(x, cot, mixa, mixb, oma, lsea, lseb, kc, wof, vec, w1, w2)
 
 
 def finish_kernel(
@@ -1302,9 +1299,13 @@
     q, k, v, attn_input, w_out_full, norms, key_code = halo_qkv(
         inputs, w_out, w_query, w_key, w_value, vec, labels
     )
-    mixed, logs = attend(bounds, q, k, v, key_code, norms, height)
-    grad_win, query_code, residual_grad, low, vectors, own1, own2, residual, out_part = mid(
-        inputs, cotangent, mixed, logs, key_code, w_out_full, vec, w_fc1, w_fc2
+    most = height // TILE - 1
+    mixed_a, logs_a = attend(bounds, q, k, v, key_code, norms, height, 0, most)
+    other_a = swapped(mixed_a)
+    mixed_a, bounds = lax.optimization_barrier((mixed_a, bounds))
+    mixed_b, logs_b = attend(bounds, q, k, v, key_code, norms, height, most, 1)
+    grad_win, query_code, residual_grad, low, vectors, own1, own2, residual, out_part, mixed = mid(
+        inputs, cotangent, mixed_a, mixed_b, other_a, logs_a, logs_b, key_code, w_out_full, vec, w_fc1, w_fc2
     )
     grad_win = grad_win.reshape(-1, grad_win.shape[2])
     out_part, query_code = lax.optimization_barrier((out_part, query_code))

time: 258 us -> 250 us (0.969); the launches traced: 262 us -> 248 us
  Pallas kernels: 250 us -> 239 us
    pallas_call x1, Pallas kernels: 91.8 us -> 79.6 us  [mid(): pl.pallas_call(mid_kernel, out_shape=(shape((blocks,) + mix.shape, BF), s...]
    pallas_call x3 -> x4, Pallas kernels: 37.2 us -> 37.1 us  [local_call(): pl.pallas_call(kernel, grid_spec=grid, out_shape=out_shape, compiler_para...]
  transfers between devices with their start and end apart: 1 -> 2, of which waited for: 1 -> 1; matrix products, arithmetic and copies ran while one was open for 0% -> 0% of each run, Pallas kernels for 9% -> 13%
where the time goes in v2:
time: 250 us; the launch traced here: 248 us
  Pallas kernels  239 us (96%)
  other arithmetic  2.74 us (1%)
    pallas_call x1, Pallas kernels, finish(): pl.pallas_call(functools.partial(finish_kernel, rounds), out_shape=(shape...  83.4 us
    pallas_call x1, Pallas kernels, mid(): pl.pallas_call(mid_kernel, out_shape=(shape((blocks,) + mix.shape, BF), s...  79.6 us
    pallas_call x4, Pallas kernels, local_call(): pl.pallas_call(kernel, grid_spec=grid, out_shape=out_shape, compiler_para...  37.1 us
    pallas_call x1, Pallas kernels, halo_qkv(): pl.pallas_call(halo_kernel, out_shape=(wide, wide, wide, shape((height, w...  33 us
    pallas_call x1, Pallas kernels, widen(): pl.pallas_call(widen_kernel, grid=(steps,), out_shape=outs, in_specs=[blo...  6.17 us
  transfers between devices with their start and end apart: 2, of which 1 were waited for; matrix products, arithmetic and copies ran while one was open for 0% of the time, Pallas kernels for 13%

profile of v2, /device:TPU:0, one launch (start us, length us, event | category | flops | bytes accessed | tf_op | source)
XLA Modules:
  0.0 248.5 jit_solution(3442438012873726061)
XLA Ops:
  0.7 0.8 convert_bitcast_fusion
  1.5 0.1 slice.44
  1.6 0.1 slice.43
  1.7 0.2 convert_reduce_fusion.1
  2.0 0.8 fusion.2
  2.8 0.9 select_select_fusion.vec_ref.row_ref
  3.6 33.0 %halo_qkv.1 = (bf16[3840,384]{1,0:T(8,128)(2,1)S(1)}, bf16[3840,384]{1,0:T(8,128)(2,1)S(1)}, bf16[3840,384]{1,0:T(8,128)(2,1)S(1)}, bf16[768,768]{1,0:T(8,128)(2...) custom-call(bf16[768,768]{1,0:T(8,128)(2,1)} %x_ref.5, ...), custom_call_target="tpu_custom_call" | custom-call | tf_op jit(solution)/shard_map/halo_qkv/pallas_call | solution.py:325
  36.7 4.5 %attend.2 = (bf16[512,384]{1,0:T(8,128)(2,1)S(1)}, f32[8,512]{1,0:T(8,128)S(1)}) custom-call(s32[2,3]{1,0:T(2,128)S(1)} %pad_add_fusion.1.b_ref, bf16[3840,384]{1,0:T(8,128)(2,1)S(1)} %get-tuple-element.62.q_ref, bf16[3840,384]{1,0:T(8,128)(2,1)S(1)} %get-tuple-element.63.k_ref, bf16[3840,384]{1,0:T(8,128)(2,1)S(1)} %get-tuple-element.64.v_ref, ...), custom_call_target="tpu_custom_call" | custom-call | tf_op jit(solution)/shard_map/attend/pallas_call | solution.py:474
  41.1 0.0 copy-start
  41.1 0.0 copy-start.4
  41.2 0.0 copy-start.6
  41.2 0.5 collective-permute-start
  41.7 5.7 %attend.3 = (bf16[256,384]{1,0:T(8,128)(2,1)S(1)}, f32[8,256]{1,0:T(8,128)S(1)}) custom-call(s32[2,3]{1,0:T(2,128)S(1)} %pad_add_fusion.1.b_ref, bf16[3840,384]{1,0:T(8,128)(2,1)S(1)} %get-tuple-element.62.q_ref, bf16[3840,384]{1,0:T(8,128)(2,1)S(1)} %get-tuple-element.63.k_ref, bf16[3840,384]{1,0:T(8,128)(2,1)S(1)} %get-tuple-element.64.v_ref, ...), custom_call_target="tpu_custom_call" | custom-call | tf_op jit(solution)/shard_map/attend/pallas_call | solution.py:474
  47.5 1.6 collective-permute-done.oma_ref
  49.0 79.6 %mid.1 = (bf16[5,768,384]{2,1,0:T(8,128)(2,1)S(1)}, bf16[3840,384]{1,0:T(8,128)(2,1)S(1)}, f32[768,768]{1,0:T(8,128)S(1)}, bf16[768,768]{1,0:T(8,128)(2,1)S(1)},...) custom-call(bf16[768,768]{1,0:T(8,128)(2,1)S(1)} %copy-done, ...), custom_call_target="tpu_custom_call" | custom-call | tf_op jit(solution)/shard_map/mid/pallas_call | solution.py:1026
  128.6 1.4 collective-permute-start.1
  130.0 12.7 %query_back.1.dq_ref = bf16[768,384]{1,0:T(8,128)(2,1)S(1)} custom-call(s32[2,3]{1,0:T(2,128)S(1)} %pad_add_fusion.1.b_ref, bf16[3840,384]{1,0:T(8,128)(2,1)S(1)} %get-tuple-element.62.q_ref, bf16[3840,384]{1,0:T(8,128)(2,1)S(1)} %get-tuple-element.63.k_ref, bf16[3840,384]{1,0:T(8,128)(2,1)S(1)} %get-tuple-element.64.v_ref, bf16[3840,384]{1,0:T(8,128)(2,1)S(1)} %bitcast.19, ...), custom_call_target="tpu_custom_call" | custom-call | tf_op jit(solution)/shard_map/query_back/pallas_call | solution.py:474
  142.8 0.0 copy-start.1
  142.8 14.2 %key_back.1 = (bf16[768,384]{1,0:T(8,128)(2,1)S(1)}, bf16[768,384]{1,0:T(8,128)(2,1)S(1)}) custom-call(s32[2,3]{1,0:T(2,128)S(1)} %pad_add_fusion.1.b_ref, bf16[3840,384]{1,0:T(8,128)(2,1)S(1)} %get-tuple-element.62.q_ref, bf16[3840,384]{1,0:T(8,128)(2,1)S(1)} %get-tuple-element.63.k_ref, bf16[3840,384]{1,0:T(8,128)(2,1)S(1)} %get-tuple-element.64.v_ref, ...), custom_call_target="tpu_custom_call" | custom-call | tf_op jit(solution)/shard_map/key_back/pallas_call | solution.py:474
  157.0 83.4 %finish.1 = (f32[768,768]{1,0:T(8,128)S(1)}, bf16[768,1536]{1,0:T(8,128)(2,1)S(1)}, f32[16,768]{1,0:T(8,128)S(1)}, bf16[768,1536]{1,0:T(8,128)(2,1)S(1)}, bf16[1...) custom-call(bf16[768,384]{1,0:T(8,128)(2,1)S(1)} %query_back.1.dq_ref, ...), custom_call_target="tpu_custom_call" | custom-call | tf_op jit(solution)/shard_map/finish/pallas_call | solution.py:1208
  240.5 6.2 %widen.1 = (f32[768,384]{1,0:T(8,128)}, f32[768,384]{1,0:T(8,128)}, f32[768,384]{1,0:T(8,128)}, f32[384,768]{1,0:T(8,128)}, f32[768,1536]{1,0:T(8,128)}, /*index...) custom-call(bf16[768,1536]{1,0:T(8,128)(2,1)S(1)} %get-tuple-element.91.a_ref, ...), custom_call_target="tpu_custom_call" | custom-call | tf_op jit(solution)/shard_map/widen/pallas_call | solution.py:1257
  246.6 0.6 slice_reduce_fusion.6
  247.2 0.6 slice_reduce_fusion
  247.9 0.6 reshape.160
  (20 shorter events, 0.1 us)
Async XLA Ops:
  41.1 7.9 %copy-start = (bf16[768,768]{1,0:T(8,128)(2,1)S(1)}, bf16[768,768]{1,0:T(8,128)(2,1)}, u32[]{:S(2)}) copy-start(bf16[768,768]{1,0:T(8,128)(2,1)} %x_ref.5) | copy-start | bytes 3538948
  41.1 7.9 %copy-start.4 = (bf16[768,1536]{1,0:T(8,128)(2,1)S(1)}, bf16[768,1536]{1,0:T(8,128)(2,1)}, u32[]{:S(2)}) copy-start(bf16[768,1536]{1,0:T(8,128)(2,1)} %w1_ref.1) | copy-start | bytes 7077892
  41.2 7.9 %copy-start.5 = (bf16[1536,768]{1,0:T(8,128)(2,1)S(1)}, bf16[1536,768]{1,0:T(8,128)(2,1)}, u32[]{:S(2)}) copy-start(bf16[1536,768]{1,0:T(8,128)(2,1)} %w2_ref.1) | copy-start | bytes 7077892
  41.2 7.9 %copy-start.6 = (bf16[768,768]{1,0:T(8,128)(2,1)S(1)}, bf16[768,768]{1,0:T(8,128)(2,1)}, u32[]{:S(2)}) copy-start(bf16[768,768]{1,0:T(8,128)(2,1)} %cot_ref.1) | copy-start | bytes 3538948
  41.2 7.8 %collective-permute-start = (bf16[512,384]{1,0:T(8,128)(2,1)S(1)}, bf16[512,384]{1,0:T(8,128)(2,1)S(1)}, u32[]{:S(2)}, u32[]{:S(2)}) collective-permute-start(bf16[512,384]{1,0:T(8,128)(2,1)S(1)} %get-tuple-element.69.mixa_ref), channel_id=1, source_target_pairs={{0,1},{1,0},{2,3},{3,2},{4,5},{5,4},{6,7},{7,6},{8,9},{9,8},{10,11... | collective-permute-start | bytes 1179656 | tf_op jit(solution)/shard_map/ppermute | solution.py:1270
  128.6 28.3 %collective-permute-start.1 = (bf16[768,768]{1,0:T(8,128)(2,1)S(1)}, bf16[768,768]{1,0:T(8,128)(2,1)S(1)}, u32[]{:S(2)}, u32[]{:S(2)}) collective-permute-start(bf16[768,768]{1,0:T(8,128)(2,1)S(1)} %get-tuple-element.78.outp_hbm), channel_id=1, source_target_pairs={{0,1},{1,0},{2,3},{3,2},{4,5},{5,4},{6,7},{7,6},{8,9},{9,8},{10,11... | collective-permute-start | bytes 3538952 | tf_op jit(solution)/shard_map/ppermute | solution.py:1270
  142.8 14.2 %copy-start.1 = (bf16[768,384]{1,0:T(8,128)(2,1)S(1)}, bf16[768,384]{1,0:T(8,128)(2,1)}, u32[]{:S(2)}) copy-start(bf16[768,384]{1,0:T(8,128)(2,1)} %wq_ref.3) | copy-start | bytes 1769476
  142.8 14.2 %copy-start.2 = (bf16[768,384]{1,0:T(8,128)(2,1)S(1)}, bf16[768,384]{1,0:T(8,128)(2,1)}, u32[]{:S(2)}) copy-start(bf16[768,384]{1,0:T(8,128)(2,1)} %wk_ref.3) | copy-start | bytes 1769476
  142.8 14.2 %copy-start.3 = (bf16[768,384]{1,0:T(8,128)(2,1)S(1)}, bf16[768,384]{1,0:T(8,128)(2,1)}, u32[]{:S(2)}) copy-start(bf16[768,384]{1,0:T(8,128)(2,1)} %wv_ref.3) | copy-start | bytes 1769476

commit v3 on v2

--- a/solution.py
+++ b/solution.py
@@ -969,6 +969,7 @@
     send(2)
     send(PARTS)
     sw_ref[REACH] = st_ref[...]
+    code(REACH)
     pass_on(0)
     ring_step(2)
     pass_on(1)
@@ -976,12 +977,22 @@
     reduce.step(hops - 1, False)
     pass_on(2)
     pass_on(PARTS)
-    code(REACH)
+    s_copy(PARTS).wait_recv()
+    code(3 - 2 * core)
+    for side in (0, 1):
+
+        @pl.when(exists[side])
+        def _():
+            code(slots[side])
+
     reduce.turn()
     own1_ref[...] = buf1[hops]
     own2_ref[...] = buf2[hops]
     for p in range(PARTS + 1):
-        s_copy(p).wait()
+        if p < PARTS:
+            s_copy(p).wait()
+        else:
+            s_copy(p).wait_send()
         for side in (0, 1):
 
             @pl.when(exists[1 - side])
@@ -996,12 +1007,7 @@
             def _():
                 f_copy(p).wait_recv()
 
-    code(3 - 2 * core)
     for side in (0, 1):
-
-        @pl.when(exists[side])
-        def _():
-            code(slots[side])
 
         @pl.when(jnp.logical_and(exists[side], core == side))
         def _():

time: 250 us -> 250 us (level); the launches traced: 248 us -> 253 us
  waiting for transfers between devices: 1.56 us -> 7.26 us
    pallas_call x4, Pallas kernels: 37.1 us -> 43.4 us  [local_call(): pl.pallas_call(kernel, grid_spec=grid, out_shape=out_shape, compiler_para...]
    ppermute x2, waiting for transfers between devices: 1.56 us -> 7.26 us  [swapped(): return lax.ppermute(value, 'tensor', [(0, 1), (1, 0)])]
    pallas_call x1, Pallas kernels: 83.4 us -> 78.8 us  [finish(): pl.pallas_call(functools.partial(finish_kernel, rounds), out_shape=(shape...]
    pallas_call x1, Pallas kernels: 79.6 us -> 76.6 us  [mid(): pl.pallas_call(mid_kernel, out_shape=(shape((blocks,) + mix.shape, BF), s...]
  transfers between devices with their start and end apart: 2 -> 2, of which waited for: 1 -> 1; matrix products, arithmetic and copies ran while one was open for 0% -> 0% of each run, Pallas kernels for 13% -> 14%
where the time goes in v3:
time: 250 us; the launch traced here: 253 us
  Pallas kernels  238 us (95%)
  waiting for transfers between devices  7.26 us (3%)
  other arithmetic  2.74 us (1%)
    pallas_call x1, Pallas kernels, finish(): pl.pallas_call(functools.partial(finish_kernel, rounds), out_shape=(shape...  78.8 us
    pallas_call x1, Pallas kernels, mid(): pl.pallas_call(mid_kernel, out_shape=(shape((blocks,) + mix.shape, BF), s...  76.6 us
    pallas_call x4, Pallas kernels, local_call(): pl.pallas_call(kernel, grid_spec=grid, out_shape=out_shape, compiler_para...  43.4 us
    pallas_call x1, Pallas kernels, halo_qkv(): pl.pallas_call(halo_kernel, out_shape=(wide, wide, wide, shape((height, w...  33 us
    ppermute x2, waiting for transfers between devices, swapped(): return lax.ppermute(value, 'tensor', [(0, 1), (1, 0)])  7.26 us
    pallas_call x1, Pallas kernels, widen(): pl.pallas_call(widen_kernel, grid=(steps,), out_shape=outs, in_specs=[blo...  6.17 us
  transfers between devices with their start and end apart: 2, of which 1 were waited for; matrix products, arithmetic and copies ran while one was open for 0% of the time, Pallas kernels for 14%

profile of v3, /device:TPU:0, one launch (start us, length us, event | category | flops | bytes accessed | tf_op | source)
XLA Modules:
  0.0 253.0 jit_solution(1471775610049384489)
XLA Ops:
  0.7 0.8 convert_bitcast_fusion
  1.5 0.1 slice.44
  1.6 0.1 slice.43
  1.7 0.2 convert_reduce_fusion.1
  2.0 0.8 fusion.2
  2.8 0.9 select_select_fusion.vec_ref.row_ref
  3.6 33.0 %halo_qkv.1 = (bf16[3840,384]{1,0:T(8,128)(2,1)S(1)}, bf16[3840,384]{1,0:T(8,128)(2,1)S(1)}, bf16[3840,384]{1,0:T(8,128)(2,1)S(1)}, bf16[768,768]{1,0:T(8,128)(2...) custom-call(bf16[768,768]{1,0:T(8,128)(2,1)} %x_ref.5, ...), custom_call_target="tpu_custom_call" | custom-call | tf_op jit(solution)/shard_map/halo_qkv/pallas_call | solution.py:325
  36.7 7.7 %attend.2 = (bf16[512,384]{1,0:T(8,128)(2,1)S(1)}, f32[8,512]{1,0:T(8,128)S(1)}) custom-call(s32[2,3]{1,0:T(2,128)S(1)} %pad_add_fusion.1.b_ref, bf16[3840,384]{1,0:T(8,128)(2,1)S(1)} %get-tuple-element.62.q_ref, bf16[3840,384]{1,0:T(8,128)(2,1)S(1)} %get-tuple-element.63.k_ref, bf16[3840,384]{1,0:T(8,128)(2,1)S(1)} %get-tuple-element.64.v_ref, ...), custom_call_target="tpu_custom_call" | custom-call | tf_op jit(solution)/shard_map/attend/pallas_call | solution.py:474
  44.4 0.0 copy-start
  44.4 0.0 copy-start.4
  44.4 0.0 copy-start.5
  44.5 0.5 collective-permute-start
  45.0 4.1 %attend.3 = (bf16[256,384]{1,0:T(8,128)(2,1)S(1)}, f32[8,256]{1,0:T(8,128)S(1)}) custom-call(s32[2,3]{1,0:T(2,128)S(1)} %pad_add_fusion.1.b_ref, bf16[3840,384]{1,0:T(8,128)(2,1)S(1)} %get-tuple-element.62.q_ref, bf16[3840,384]{1,0:T(8,128)(2,1)S(1)} %get-tuple-element.63.k_ref, bf16[3840,384]{1,0:T(8,128)(2,1)S(1)} %get-tuple-element.64.v_ref, ...), custom_call_target="tpu_custom_call" | custom-call | tf_op jit(solution)/shard_map/attend/pallas_call | solution.py:474
  49.1 7.3 %collective-permute-done.oma_ref = bf16[512,384]{1,0:T(8,128)(2,1)S(1)} collective-permute-done((bf16[512,384]{1,0:T(8,128)(2,1)S(1)}, bf16[512,384]{1,0:T(8,128)(2,1)S(1)}, u32[]{:S(2)}, u32[]{:S(2)}) %collective-permute-start) | collective-permute-done | bytes 393248 | tf_op jit(solution)/shard_map/ppermute | solution.py:1276
  56.4 76.6 %mid.1 = (bf16[5,768,384]{2,1,0:T(8,128)(2,1)S(1)}, bf16[3840,384]{1,0:T(8,128)(2,1)S(1)}, f32[768,768]{1,0:T(8,128)S(1)}, bf16[768,768]{1,0:T(8,128)(2,1)S(1)},...) custom-call(bf16[768,768]{1,0:T(8,128)(2,1)S(1)} %copy-done, ...), custom_call_target="tpu_custom_call" | custom-call | tf_op jit(solution)/shard_map/mid/pallas_call | solution.py:1032
  133.0 1.6 collective-permute-start.1
  134.5 14.9 %query_back.1.dq_ref = bf16[768,384]{1,0:T(8,128)(2,1)S(1)} custom-call(s32[2,3]{1,0:T(2,128)S(1)} %pad_add_fusion.1.b_ref, bf16[3840,384]{1,0:T(8,128)(2,1)S(1)} %get-tuple-element.62.q_ref, bf16[3840,384]{1,0:T(8,128)(2,1)S(1)} %get-tuple-element.63.k_ref, bf16[3840,384]{1,0:T(8,128)(2,1)S(1)} %get-tuple-element.64.v_ref, bf16[3840,384]{1,0:T(8,128)(2,1)S(1)} %bitcast.19, ...), custom_call_target="tpu_custom_call" | custom-call | tf_op jit(solution)/shard_map/query_back/pallas_call | solution.py:474
  149.5 0.0 copy-start.1
  149.5 16.6 %key_back.1 = (bf16[768,384]{1,0:T(8,128)(2,1)S(1)}, bf16[768,384]{1,0:T(8,128)(2,1)S(1)}) custom-call(s32[2,3]{1,0:T(2,128)S(1)} %pad_add_fusion.1.b_ref, bf16[3840,384]{1,0:T(8,128)(2,1)S(1)} %get-tuple-element.62.q_ref, bf16[3840,384]{1,0:T(8,128)(2,1)S(1)} %get-tuple-element.63.k_ref, bf16[3840,384]{1,0:T(8,128)(2,1)S(1)} %get-tuple-element.64.v_ref, ...), custom_call_target="tpu_custom_call" | custom-call | tf_op jit(solution)/shard_map/key_back/pallas_call | solution.py:474
  166.2 78.8 %finish.1 = (f32[768,768]{1,0:T(8,128)S(1)}, bf16[768,1536]{1,0:T(8,128)(2,1)S(1)}, f32[16,768]{1,0:T(8,128)S(1)}, bf16[768,1536]{1,0:T(8,128)(2,1)S(1)}, bf16[1...) custom-call(bf16[768,384]{1,0:T(8,128)(2,1)S(1)} %query_back.1.dq_ref, ...), custom_call_target="tpu_custom_call" | custom-call | tf_op jit(solution)/shard_map/finish/pallas_call | solution.py:1214
  245.0 6.2 %widen.1 = (f32[768,384]{1,0:T(8,128)}, f32[768,384]{1,0:T(8,128)}, f32[768,384]{1,0:T(8,128)}, f32[384,768]{1,0:T(8,128)}, f32[768,1536]{1,0:T(8,128)}, /*index...) custom-call(bf16[768,1536]{1,0:T(8,128)(2,1)S(1)} %get-tuple-element.91.a_ref, ...), custom_call_target="tpu_custom_call" | custom-call | tf_op jit(solution)/shard_map/widen/pallas_call | solution.py:1263
  251.2 0.6 slice_reduce_fusion.6
  251.8 0.6 slice_reduce_fusion
  252.4 0.6 reshape.160
  (20 shorter events, 0.1 us)
Async XLA Ops:
  44.4 12.0 %copy-start = (bf16[768,768]{1,0:T(8,128)(2,1)S(1)}, bf16[768,768]{1,0:T(8,128)(2,1)}, u32[]{:S(2)}) copy-start(bf16[768,768]{1,0:T(8,128)(2,1)} %x_ref.5) | copy-start | bytes 3538948
  44.4 12.0 %copy-start.4 = (bf16[768,1536]{1,0:T(8,128)(2,1)S(1)}, bf16[768,1536]{1,0:T(8,128)(2,1)}, u32[]{:S(2)}) copy-start(bf16[768,1536]{1,0:T(8,128)(2,1)} %w1_ref.1) | copy-start | bytes 7077892
  44.4 11.9 %copy-start.5 = (bf16[1536,768]{1,0:T(8,128)(2,1)S(1)}, bf16[1536,768]{1,0:T(8,128)(2,1)}, u32[]{:S(2)}) copy-start(bf16[1536,768]{1,0:T(8,128)(2,1)} %w2_ref.1) | copy-start | bytes 7077892
  44.4 11.9 %copy-start.6 = (bf16[768,768]{1,0:T(8,128)(2,1)S(1)}, bf16[768,768]{1,0:T(8,128)(2,1)}, u32[]{:S(2)}) copy-start(bf16[768,768]{1,0:T(8,128)(2,1)} %cot_ref.1) | copy-start | bytes 3538948
  44.5 11.9 %collective-permute-start = (bf16[512,384]{1,0:T(8,128)(2,1)S(1)}, bf16[512,384]{1,0:T(8,128)(2,1)S(1)}, u32[]{:S(2)}, u32[]{:S(2)}) collective-permute-start(bf16[512,384]{1,0:T(8,128)(2,1)S(1)} %get-tuple-element.69.mixa_ref), channel_id=1, source_target_pairs={{0,1},{1,0},{2,3},{3,2},{4,5},{5,4},{6,7},{7,6},{8,9},{9,8},{10,11... | collective-permute-start | bytes 1179656 | tf_op jit(solution)/shard_map/ppermute | solution.py:1276
  133.0 33.2 %collective-permute-start.1 = (bf16[768,768]{1,0:T(8,128)(2,1)S(1)}, bf16[768,768]{1,0:T(8,128)(2,1)S(1)}, u32[]{:S(2)}, u32[]{:S(2)}) collective-permute-start(bf16[768,768]{1,0:T(8,128)(2,1)S(1)} %get-tuple-element.78.outp_hbm), channel_id=1, source_target_pairs={{0,1},{1,0},{2,3},{3,2},{4,5},{5,4},{6,7},{7,6},{8,9},{9,8},{10,11... | collective-permute-start | bytes 3538952 | tf_op jit(solution)/shard_map/ppermute | solution.py:1276
  149.5 16.7 %copy-start.1 = (bf16[768,384]{1,0:T(8,128)(2,1)S(1)}, bf16[768,384]{1,0:T(8,128)(2,1)}, u32[]{:S(2)}) copy-start(bf16[768,384]{1,0:T(8,128)(2,1)} %wq_ref.3) | copy-start | bytes 1769476
  149.5 16.7 %copy-start.2 = (bf16[768,384]{1,0:T(8,128)(2,1)S(1)}, bf16[768,384]{1,0:T(8,128)(2,1)}, u32[]{:S(2)}) copy-start(bf16[768,384]{1,0:T(8,128)(2,1)} %wk_ref.3) | copy-start | bytes 1769476
  149.5 16.7 %copy-start.3 = (bf16[768,384]{1,0:T(8,128)(2,1)S(1)}, bf16[768,384]{1,0:T(8,128)(2,1)}, u32[]{:S(2)}) copy-start(bf16[768,384]{1,0:T(8,128)(2,1)} %wv_ref.3) | copy-start | bytes 1769476
